TPU v7x, 32 devices: a whole 2x2x4 slice. The times are simulated.
32 devices in a mesh: cuts: 4 (over z), tile: 2 (over core), probe: 4 (over y, x).
Axes of the slice: x: 2, y: 2, z: 4, core: 2. Of those that a mesh axis runs over, the one named last changes fastest.
Arguments:
- probe_wave: bfloat16 [2, 512, 512], replicated, may hold values from -6 to 6
- fresnel_rows: bfloat16 [2, 512, 512], replicated, may hold values from -0.1875 to 0.1875
- fresnel_cols: bfloat16 [2, 512, 512], replicated, may hold values from -0.1875 to 0.1875
- object_slices: float32 [4, 2, 1024, 768], P('cuts', None, 'tile'), may hold values from -1 to 1.9, as said below
- offsets: int32 [2, 8, 2], P('tile', 'probe'), may hold values from 0 to 256
- measured: float32 [2, 8, 512, 512], P('tile', 'probe'), may hold values from 0.2 to 2
Outputs:
- updated_object: float32 [4, 2, 1024, 768], P('cuts', None, ('tile', 'probe'))
Inputs may be any that keep to these rules, and one draw needn't show every extreme that they name: `object_slices`: real and imaginary parts of each slice's transmission.
All inputs are finite; a program needn't handle non-finite values.
Results may differ from a plain program's by a relative error of at most 0.02.
Values may be sent and summed in bfloat16 or wider, within the bound.
No kernel may reach another device: no remote copies, remote signals or barrier semaphores. Data moves between devices by JAX's collectives and lax.ppermute only.
A program may use at most 128 MiB of HBM per device.

v0:
```python
import jax
import jax.numpy as jnp
from jax import lax
from jax.sharding import PartitionSpec as P

MARGIN = 128


def extended_2(x, sides, width):
    for axis, dim in sides:
        count, length = (lax.axis_size(axis), x.shape[dim])
        up = [(i, (i + 1) % count) for i in range(count)]
        down = [(j, i) for i, j in up]
        last = lax.slice_in_dim(x, length - width, length, axis=dim)
        leading = lax.slice_in_dim(x, 0, width, axis=dim)
        before = lax.ppermute(last, axis, up)
        after = lax.ppermute(leading, axis, down)
        x = jnp.concatenate([before, x, after], axis=dim)
    return x


def passed_along(x, axis, by):
    count = lax.axis_size(axis)
    pairs = [(i, i + by) for i in range(count) if 0 <= i + by < count]
    return lax.ppermute(x, axis, pairs)


def complex_mul(left_side, right_side):
    return jnp.stack(
        [
            left_side[:, 0] * right_side[:, 0] - left_side[:, 1] * right_side[:, 1],
            left_side[:, 0] * right_side[:, 1] + left_side[:, 1] * right_side[:, 0],
        ],
        axis=1,
    )


def conj_mul(left_side, right_side):
    return jnp.stack(
        [
            left_side[:, 0] * right_side[:, 0] + left_side[:, 1] * right_side[:, 1],
            left_side[:, 0] * right_side[:, 1] - left_side[:, 1] * right_side[:, 0],
        ],
        axis=1,
    )


def times_transposed(stacked, matrix):
    return lax.dot_general(
        stacked, matrix, (((1,), (1,)), ((), ())), preferred_element_type=jnp.float32
    )


def forward_apply(wave, col_real, col_imag, left_block):
    size = wave.shape[1]
    stacked = wave.reshape(2 * size, size)
    with_real = times_transposed(stacked, col_real)
    with_imag = times_transposed(stacked, col_imag)
    mid_real = with_real[:size] - with_imag[size:]
    mid_imag = with_imag[:size] + with_real[size:]
    middle = jnp.concatenate([mid_real, mid_imag], axis=0).astype(jnp.bfloat16)
    result = jnp.dot(left_block, middle, preferred_element_type=jnp.float32)
    return result.astype(jnp.bfloat16).reshape(2, size, size)


def adjoint_apply(wave, col_real, col_imag, left_block):
    size = wave.shape[1]
    stacked = wave.reshape(2 * size, size)
    with_real = jnp.dot(stacked, col_real, preferred_element_type=jnp.float32)
    with_imag = jnp.dot(stacked, col_imag, preferred_element_type=jnp.float32)
    mid_real = with_real[:size] + with_imag[size:]
    mid_imag = with_real[size:] - with_imag[:size]
    middle = jnp.concatenate([mid_real, mid_imag], axis=0).astype(jnp.bfloat16)
    result = jnp.dot(left_block, middle, preferred_element_type=jnp.float32)
    return result.astype(jnp.bfloat16).reshape(2, size, size)


def shards(probe_wave, fresnel_rows, fresnel_cols, object_slices, offsets, measured):
    cut_count = lax.axis_size("cuts")
    section_index = lax.axis_index("cuts")
    owned = object_slices[0]
    own_count = owned.shape[1]
    width_cols = owned.shape[2]
    window_size = probe_wave.shape[1]
    transmission = owned.astype(jnp.bfloat16)
    extended = extended_2(transmission, (("tile", 1),), MARGIN)
    starts = offsets[0]
    position_count = starts.shape[0]

    def cut_window(row_start, col_start):
        return lax.dynamic_slice(
            extended, (jnp.int32(0), row_start, col_start), (2, window_size, window_size)
        )

    windows = jax.vmap(cut_window)(starts[:, 0], starts[:, 1])
    row_real, row_imag = (fresnel_rows[0], fresnel_rows[1])
    col_real, col_imag = (fresnel_cols[0], fresnel_cols[1])
    forward_left = jnp.concatenate(
        [
            jnp.concatenate([row_real, -row_imag], axis=1),
            jnp.concatenate([row_imag, row_real], axis=1),
        ],
        axis=0,
    )
    adjoint_left = jnp.concatenate(
        [
            jnp.concatenate([row_real.T, row_imag.T], axis=1),
            jnp.concatenate([-row_imag.T, row_real.T], axis=1),
        ],
        axis=0,
    )
    wave_shape = (2, window_size, window_size)
    tick_count = cut_count + position_count - 1
    last_section = cut_count - 1

    def advance(wave, window):
        exits = complex_mul(
            wave[None].astype(jnp.float32), window[None].astype(jnp.float32)
        ).astype(jnp.bfloat16)
        return forward_apply(exits[0], col_real, col_imag, forward_left)

    def standby(wave, window):
        return jnp.zeros_like(wave)

    def forward_tick(tick, carry):
        incoming, saved, finals = carry
        position = tick - section_index
        valid = (position >= 0) & (position < position_count)
        slot = jnp.clip(position, 0, position_count - 1)
        wave_in = jnp.where(section_index == 0, probe_wave, incoming)
        window = lax.dynamic_index_in_dim(windows, slot, 0, keepdims=False)
        produced = lax.cond(valid, advance, standby, wave_in, window)
        previous = lax.dynamic_index_in_dim(saved, slot, 0, keepdims=False)
        saved = lax.dynamic_update_index_in_dim(saved, jnp.where(valid, wave_in, previous), slot, 0)
        earlier = lax.dynamic_index_in_dim(finals, slot, 0, keepdims=False)
        keep_final = valid & (section_index == last_section)
        finals = lax.dynamic_update_index_in_dim(
            finals, jnp.where(keep_final, produced, earlier), slot, 0
        )
        incoming = passed_along(produced, "cuts", 1)
        return (incoming, saved, finals)

    start_wave = jnp.zeros(wave_shape, jnp.bfloat16)
    stack_zeros = jnp.zeros((position_count,) + wave_shape, jnp.bfloat16)
    _, saved, finals = lax.fori_loop(
        0, tick_count, forward_tick, (start_wave, stack_zeros, stack_zeros)
    )
    psi_final = finals.astype(jnp.float32)
    amplitude = measured[0]
    factor = 1.0 - amplitude / jnp.sqrt(psi_final[:, 0] ** 2 + psi_final[:, 1] ** 2 + 1.0)
    final_cots = (psi_final * factor[:, None]).astype(jnp.bfloat16)

    def retreat(cotangent, window, wave_before):
        backed = adjoint_apply(cotangent, col_real, col_imag, adjoint_left)[None].astype(
            jnp.float32
        )
        incoming = wave_before[None].astype(jnp.float32)
        gradient_term = conj_mul(incoming, backed)[0]
        intensity = incoming[0, 0] ** 2 + incoming[0, 1] ** 2
        sending = conj_mul(window[None].astype(jnp.float32), backed).astype(jnp.bfloat16)[0]
        return (sending, gradient_term, intensity)

    def resting(cotangent, window, wave_before):
        zeros_wave = jnp.zeros(wave_shape, jnp.float32)
        zeros_light = jnp.zeros((window_size, window_size), jnp.float32)
        return (jnp.zeros_like(cotangent), zeros_wave, zeros_light)

    def backward_tick(tick, carry):
        incoming, gradient_total, light_total = carry
        position = tick - (last_section - section_index)
        valid = (position >= 0) & (position < position_count)
        slot = jnp.clip(position, 0, position_count - 1)
        own_cot = lax.dynamic_index_in_dim(final_cots, slot, 0, keepdims=False)
        cot_in = jnp.where(section_index == last_section, own_cot, incoming)
        window = lax.dynamic_index_in_dim(windows, slot, 0, keepdims=False)
        wave_before = lax.dynamic_index_in_dim(saved, slot, 0, keepdims=False)
        sending, gradient_term, intensity = lax.cond(
            valid, retreat, resting, cot_in, window, wave_before
        )
        gradient_old = lax.dynamic_index_in_dim(gradient_total, slot, 0, keepdims=False)
        gradient_total = lax.dynamic_update_index_in_dim(
            gradient_total, gradient_old + gradient_term, slot, 0
        )
        light_old = lax.dynamic_index_in_dim(light_total, slot, 0, keepdims=False)
        light_total = lax.dynamic_update_index_in_dim(light_total, light_old + intensity, slot, 0)
        incoming = passed_along(sending, "cuts", -1)
        return (incoming, gradient_total, light_total)

    gradient_start = jnp.zeros((position_count,) + wave_shape, jnp.float32)
    light_start = jnp.zeros((position_count, window_size, window_size), jnp.float32)
    _, gradient_total, light_total = lax.fori_loop(
        0, tick_count, backward_tick, (start_wave, gradient_start, light_start)
    )
    pieces = jnp.concatenate([gradient_total, light_total[:, None]], axis=1)
    accum_grid = jnp.zeros((3, own_count + 2 * MARGIN, width_cols), jnp.float32)
    for position in range(position_count):
        anchor = (jnp.int32(0), starts[position, 0], starts[position, 1])
        current_block = lax.dynamic_slice(accum_grid, anchor, (3, window_size, window_size))
        accum_grid = lax.dynamic_update_slice(accum_grid, current_block + pieces[position], anchor)
    edged = extended_2(accum_grid.astype(jnp.bfloat16), (("tile", 1),), MARGIN).astype(
        accum_grid.dtype
    )
    inside = accum_grid[:, MARGIN : MARGIN + own_count]
    upper_rows = inside[:, :MARGIN] + edged[:, :MARGIN]
    lower_rows = inside[:, own_count - MARGIN :] + edged[:, edged.shape[1] - MARGIN :]
    folded = jnp.concatenate(
        [upper_rows, inside[:, MARGIN : own_count - MARGIN], lower_rows], axis=1
    )
    summed = lax.psum_scatter(
        folded.astype(jnp.bfloat16), "probe", scatter_dimension=1, tiled=True
    ).astype(jnp.float32)
    rows_each = summed.shape[1]
    own_part = lax.dynamic_slice_in_dim(owned, lax.axis_index("probe") * rows_each, rows_each, 1)
    updated = own_part - summed[:2] / (summed[2] + 1.0)
    return updated[None]


def solution(mesh):
    in_specs = (
        P(),
        P(),
        P(),
        P("cuts", None, "tile", None),
        P("tile", "probe", None),
        P("tile", "probe", None, None),
    )
    out_specs = P("cuts", None, ("tile", "probe"), None)
    return jax.shard_map(shards, mesh=mesh, in_specs=in_specs, out_specs=out_specs, check_vma=False)
```

profile of v0, /device:TPU:0, one launch (start us, length us, event | category | flops | bytes accessed | tf_op | source)
XLA Modules:
  0.0 580.5 jit_solution(3615901670088689353)
XLA Ops:
  21.2 2.6 copy.32
  23.8 3.8 copy.31
  34.5 7.1 %while.40 = (s32[]{:T(128)}, bf16[2,768,768]{2,1,0:T(8,128)(2,1)S(1)}, s32[2,3]{1,0:T(2,128)S(1)}, bf16[2,2,512,512]{3,2,1,0:T(8,128)(2,1)}, s32[]{:T(128)}) while((s32[]{:T(128)}, bf16[2,768,768]{2,1,0:T(8,128)(2,1)S(1)}, s32[2,3]{1,0:T(2,128)S(1)}, bf16[2,2,512,512]{3,2,1,0:T(8,128)(2,1)}, s32[]{:T(128)}) %tuple.138), condition=%wide.while_cond, body=%wide.while_body.sunk | while | flops 2 | bytes 2098793 | solution.py:91
  35.2 2.9 bitcast_dynamic-update-slice_fusion.8
  38.7 2.9 bitcast_dynamic-update-slice_fusion.8
  46.3 201.7 %while.38 = (s32[]{:T(128)}, bf16[2,512,512]{1,0,2:T(2,128)(2,1)}, bf16[2,2,512,512]{3,2,1,0:T(8,128)(2,1)}, bf16[2,2,512,512]{3,2,1,0:T(8,128)(2,1)}, s32[]{:T(...) while((s32[]{:T(128)}, bf16[2,512,512]{1,0,2:T(2,128)(2,1)}, ...), condition=%wide.region_3.4_spmd, body=%wide.region_0.3_spmd.sunk | while | flops 2156396544 | bytes 72352600 | solution.py:145
  48.6 3.7 fusion.54
  52.3 11.2 %conditional.4 = (bf16[2,512,512]{1,0,2:T(2,128)(2,1)S(1)}) conditional(s32[]{:T(128)} %convert_element_type.147, () %tuple.129, (bf16[2,512,512]{1,0,2:T(2,128)(2,1)S(1)}, bf16[2,2,512,512]{3,2,1,0:T(8,128)(2,1)}, s32[]{:T(128)}, bf16[512,512]{1,0:T(8,128)(2,1)}, bf16[512,512]{1,0:T(8,128)(2,1)}, /*index=5*/bf16[1024,1024]{1,0:T(8,128)(2,1)}) %tuple.130), branch_computations={%region_1.1_spmd, %region_2.2_spmd} | conditional | flops 2154823680 | bytes 42991656 | solution.py:132
  70.7 2.5 copy.51
  74.6 13.6 %collective-permute-done = bf16[2,512,512]{1,0,2:T(2,128)(2,1)} collective-permute-done((bf16[2,512,512]{1,0,2:T(2,128)(2,1)S(1)}, bf16[2,512,512]{1,0,2:T(2,128)(2,1)}, u32[]{:S(2)}, u32[]{:S(2)}) %collective-permute-start) | collective-permute-done | bytes 1048608 | tf_op jit(solution)/shard_map/while/body/eval_jaxpr/ppermute | solution.py:25
  90.5 3.7 fusion.54
  94.2 11.2 %conditional.4 = (bf16[2,512,512]{1,0,2:T(2,128)(2,1)S(1)}) conditional(s32[]{:T(128)} %convert_element_type.147, () %tuple.129, (bf16[2,512,512]{1,0,2:T(2,128)(2,1)S(1)}, bf16[2,2,512,512]{3,2,1,0:T(8,128)(2,1)}, s32[]{:T(128)}, bf16[512,512]{1,0:T(8,128)(2,1)}, bf16[512,512]{1,0:T(8,128)(2,1)}, /*index=5*/bf16[1024,1024]{1,0:T(8,128)(2,1)}) %tuple.130), branch_computations={%region_1.1_spmd, %region_2.2_spmd} | conditional | flops 2154823680 | bytes 42991656 | solution.py:132
  105.4 5.5 collective-permute-start
  115.8 2.5 copy.51
  119.8 12.7 %collective-permute-done = bf16[2,512,512]{1,0,2:T(2,128)(2,1)} collective-permute-done((bf16[2,512,512]{1,0,2:T(2,128)(2,1)S(1)}, bf16[2,512,512]{1,0,2:T(2,128)(2,1)}, u32[]{:S(2)}, u32[]{:S(2)}) %collective-permute-start) | collective-permute-done | bytes 1048608 | tf_op jit(solution)/shard_map/while/body/eval_jaxpr/ppermute | solution.py:25
  134.7 3.7 fusion.54
  139.0 16.2 %collective-permute-start = (bf16[2,512,512]{1,0,2:T(2,128)(2,1)S(1)}, bf16[2,512,512]{1,0,2:T(2,128)(2,1)}, u32[]{:S(2)}, u32[]{:S(2)}) collective-permute-start(bf16[2,512,512]{1,0,2:T(2,128)(2,1)S(1)} %get-tuple-element.1083), channel_id=1, source_target_pairs={{0,8},{8,16},{16,24},{1,9},{9,17},{17,25},{2,10},{10,18},{18,26},{... | collective-permute-start | bytes 3145736 | tf_op jit(solution)/shard_map/while/body/eval_jaxpr/ppermute | solution.py:25
  160.0 2.5 copy.51
  164.0 11.8 %collective-permute-done = bf16[2,512,512]{1,0,2:T(2,128)(2,1)} collective-permute-done((bf16[2,512,512]{1,0,2:T(2,128)(2,1)S(1)}, bf16[2,512,512]{1,0,2:T(2,128)(2,1)}, u32[]{:S(2)}, u32[]{:S(2)}) %collective-permute-start) | collective-permute-done | bytes 1048608 | tf_op jit(solution)/shard_map/while/body/eval_jaxpr/ppermute | solution.py:25
  178.1 3.7 fusion.54
  182.4 5.5 collective-permute-start
  192.8 2.5 copy.51
  196.7 11.0 %collective-permute-done = bf16[2,512,512]{1,0,2:T(2,128)(2,1)} collective-permute-done((bf16[2,512,512]{1,0,2:T(2,128)(2,1)S(1)}, bf16[2,512,512]{1,0,2:T(2,128)(2,1)}, u32[]{:S(2)}, u32[]{:S(2)}) %collective-permute-start) | collective-permute-done | bytes 1048608 | tf_op jit(solution)/shard_map/while/body/eval_jaxpr/ppermute | solution.py:25
  210.0 3.7 fusion.54
  214.3 14.4 %collective-permute-start = (bf16[2,512,512]{1,0,2:T(2,128)(2,1)S(1)}, bf16[2,512,512]{1,0,2:T(2,128)(2,1)}, u32[]{:S(2)}, u32[]{:S(2)}) collective-permute-start(bf16[2,512,512]{1,0,2:T(2,128)(2,1)S(1)} %get-tuple-element.1083), channel_id=1, source_target_pairs={{0,8},{8,16},{16,24},{1,9},{9,17},{17,25},{2,10},{10,18},{18,26},{... | collective-permute-start | bytes 3145736 | tf_op jit(solution)/shard_map/while/body/eval_jaxpr/ppermute | solution.py:25
  233.6 2.5 copy.51
  237.5 10.4 %collective-permute-done = bf16[2,512,512]{1,0,2:T(2,128)(2,1)} collective-permute-done((bf16[2,512,512]{1,0,2:T(2,128)(2,1)S(1)}, bf16[2,512,512]{1,0,2:T(2,128)(2,1)}, u32[]{:S(2)}, u32[]{:S(2)}) %collective-permute-start) | collective-permute-done | bytes 1048608 | tf_op jit(solution)/shard_map/while/body/eval_jaxpr/ppermute | solution.py:25
  253.7 2.6 broadcast_in_dim.61
  258.9 213.6 %while.39 = (s32[]{:T(128)}, bf16[2,512,512]{2,1,0:T(8,128)(2,1)}, f32[2,2,512,512]{3,2,1,0:T(8,128)}, f32[2,512,512]{2,1,0:T(8,128)}, s32[]{:T(128)}, /*index=5...) while((s32[]{:T(128)}, bf16[2,512,512]{2,1,0:T(8,128)(2,1)}, ...), condition=%wide.region_7.8_spmd, body=%wide.region_4.7_spmd.sunk | while | flops 2159542272 | bytes 118489544 | solution.py:191
  258.9 2.8 conditional.5
  269.5 17.1 %collective-permute-done.1 = bf16[2,512,512]{2,1,0:T(8,128)(2,1)} collective-permute-done((bf16[2,512,512]{2,1,0:T(8,128)(2,1)}, bf16[2,512,512]{2,1,0:T(8,128)(2,1)}, u32[]{:S(2)}, u32[]{:S(2)}) %collective-permute-start.1) | collective-permute-done | bytes 1048608 | tf_op jit(solution)/shard_map/while/body/eval_jaxpr/ppermute | solution.py:25
  286.6 2.8 conditional.5
  297.2 26.0 %collective-permute-done.1 = bf16[2,512,512]{2,1,0:T(8,128)(2,1)} collective-permute-done((bf16[2,512,512]{2,1,0:T(8,128)(2,1)}, bf16[2,512,512]{2,1,0:T(8,128)(2,1)}, u32[]{:S(2)}, u32[]{:S(2)}) %collective-permute-start.1) | collective-permute-done | bytes 1048608 | tf_op jit(solution)/shard_map/while/body/eval_jaxpr/ppermute | solution.py:25
  323.2 2.8 conditional.5
  333.8 59.3 %collective-permute-done.1 = bf16[2,512,512]{2,1,0:T(8,128)(2,1)} collective-permute-done((bf16[2,512,512]{2,1,0:T(8,128)(2,1)}, bf16[2,512,512]{2,1,0:T(8,128)(2,1)}, u32[]{:S(2)}, u32[]{:S(2)}) %collective-permute-start.1) | collective-permute-done | bytes 1048608 | tf_op jit(solution)/shard_map/while/body/eval_jaxpr/ppermute | solution.py:25
  393.2 17.5 %conditional.5 = (bf16[2,512,512]{2,1,0:T(8,128)(2,1)}, f32[2,512,512]{2,1,0:T(8,128)}, f32[512,512]{1,0:T(8,128)S(1)}) conditional(s32[]{:T(128)} %convert_element_type.148, () %tuple.132, (bf16[2,2,512,512]{3,2,1,0:T(8,128)(2,1)}, s32[]{:T(128)}, pred[]{:T(512)}, bf16[2,2,512,512]{3,2,1,0:T(8,128)(2,1)}, bf16[2,512,512]{2,1,0:T(8,128)(2,1)}, ...), branch_computations={%region_5.5_spmd, %region_6.6_spmd} | conditional | flops 2158755840 | bytes 48234528 | solution.py:177
  398.9 4.2 convert_bitcast_fusion
  418.5 14.7 %collective-permute-done.1 = bf16[2,512,512]{2,1,0:T(8,128)(2,1)} collective-permute-done((bf16[2,512,512]{2,1,0:T(8,128)(2,1)}, bf16[2,512,512]{2,1,0:T(8,128)(2,1)}, u32[]{:S(2)}, u32[]{:S(2)}) %collective-permute-start.1) | collective-permute-done | bytes 1048608 | tf_op jit(solution)/shard_map/while/body/eval_jaxpr/ppermute | solution.py:25
  433.2 17.5 %conditional.5 = (bf16[2,512,512]{2,1,0:T(8,128)(2,1)}, f32[2,512,512]{2,1,0:T(8,128)}, f32[512,512]{1,0:T(8,128)S(1)}) conditional(s32[]{:T(128)} %convert_element_type.148, () %tuple.132, (bf16[2,2,512,512]{3,2,1,0:T(8,128)(2,1)}, s32[]{:T(128)}, pred[]{:T(512)}, bf16[2,2,512,512]{3,2,1,0:T(8,128)(2,1)}, bf16[2,512,512]{2,1,0:T(8,128)(2,1)}, ...), branch_computations={%region_5.5_spmd, %region_6.6_spmd} | conditional | flops 2158755840 | bytes 48234528 | solution.py:177
  439.0 4.2 convert_bitcast_fusion
  458.6 13.9 %collective-permute-done.1 = bf16[2,512,512]{2,1,0:T(8,128)(2,1)} collective-permute-done((bf16[2,512,512]{2,1,0:T(8,128)(2,1)}, bf16[2,512,512]{2,1,0:T(8,128)(2,1)}, u32[]{:S(2)}, u32[]{:S(2)}) %collective-permute-start.1) | collective-permute-done | bytes 1048608 | tf_op jit(solution)/shard_map/while/body/eval_jaxpr/ppermute | solution.py:25
  472.5 3.9 fusion.18
  476.4 3.4 broadcast_in_dim.60
  479.8 17.8 %dynamic_update_slice.43 = f32[3,768,768]{2,1,0:T(8,128)} dynamic-update-slice(f32[3,768,768]{2,1,0:T(8,128)} %broadcast_in_dim.60, f32[3,512,512]{2,1,0:T(8,128)} %fusion.18, s32[]{:T(128)} %constant.151.clone.1, s32[]{:T(128)S(6)} %select_n.122, s32[]{:T(128)S(6)} %select_n.123) | dynamic-update-slice | bytes 6291460 | tf_op jit(solution)/shard_map/dynamic_update_slice | solution.py:199
  497.6 5.4 fusion.20
  503.0 21.8 %dynamic_update_slice.44 = f32[3,768,768]{2,1,0:T(8,128)} dynamic-update-slice(f32[3,768,768]{2,1,0:T(8,128)} %dynamic_update_slice.43, f32[3,512,512]{2,1,0:T(8,128)} %fusion.20, s32[]{:T(128)} %constant.151.clone.1, s32[]{:T(128)S(6)} %select_n.124, s32[]{:T(128)S(6)} %select_n.125) | dynamic-update-slice | bytes 6291460 | tf_op jit(solution)/shard_map/dynamic_update_slice | solution.py:199
  524.8 3.4 convert_element_type.121
  534.7 35.7 %reduce-scatter.2.cloned.1.call-done = bf16[3,128,768]{2,1,0:T(8,128)(2,1)} async-done(((bf16[3,512,768]{2,1,0:T(8,128)(2,1)}), bf16[3,128,768]{2,1,0:T(8,128)(2,1)}) %reduce-scatter.2.cloned.1.call-update) | async-done | bytes 589840 | tf_op jit(solution)/shard_map/reduce_scatter | solution.py:209
  (219 shorter events, 182.7 us)
Async XLA Ops:
  6.5 3.7 copy-start.10
  6.5 563.8 %reduce-scatter.2.cloned.1.call-start = ((), (), s32[]{:S(2)}) async-start(), calls=%async_computation.1 | async-start | bytes 2949120 | tf_op jit(solution)/shard_map/reduce_scatter | solution.py:209
  8.7 1.6 copy-start.6
  9.7 21.5 %collective-permute-start.2 = (bf16[2,128,768]{2,1,0:T(8,128)(2,1)}, bf16[2,128,768]{2,1,0:T(8,128)(2,1)S(1)}, u32[]{:S(2)}, u32[]{:S(2)}) collective-permute-start(bf16[2,128,768]{2,1,0:T(8,128)(2,1)} %get-tuple-element.771), channel_id=1, source_target_pairs={{0,4},{4,0},{1,5},{5,1},{2,6},{6,2},{3,7},{7,3},{8,12},{12,8},{9,1... | collective-permute-start | bytes 1179656 | tf_op jit(solution)/shard_map/ppermute | solution.py:16
  10.2 21.0 %collective-permute-start.3 = (bf16[2,128,768]{2,1,0:T(8,128)(2,1)}, bf16[2,128,768]{2,1,0:T(8,128)(2,1)}, u32[]{:S(2)}, u32[]{:S(2)}) collective-permute-start(bf16[2,128,768]{2,1,0:T(8,128)(2,1)} %get-tuple-element.772), channel_id=1, source_target_pairs={{4,0},{0,4},{5,1},{1,5},{6,2},{2,6},{7,3},{3,7},{12,8},{8,12},{13,... | collective-permute-start | bytes 1179656 | tf_op jit(solution)/shard_map/ppermute | solution.py:17
  10.3 1.9 copy-start.12
  12.5 1.4 copy-start.7
  23.8 6.4 %copy-start.11 = (bf16[2,512,512]{2,1,0:T(8,128)(2,1)S(1)}, bf16[2,512,512]{2,1,0:T(8,128)(2,1)}, u32[]{:S(2)}) copy-start(bf16[2,512,512]{2,1,0:T(8,128)(2,1)} %param.16) | copy-start | bytes 3145732
  59.8 1.6 copy-start.8
  63.5 24.6 %collective-permute-start = (bf16[2,512,512]{1,0,2:T(2,128)(2,1)S(1)}, bf16[2,512,512]{1,0,2:T(2,128)(2,1)}, u32[]{:S(2)}, u32[]{:S(2)}) collective-permute-start(bf16[2,512,512]{1,0,2:T(2,128)(2,1)S(1)} %get-tuple-element.1083), channel_id=1, source_target_pairs={{0,8},{8,16},{16,24},{1,9},{9,17},{17,25},{2,10},{10,18},{18,26},{... | collective-permute-start | bytes 3145736 | tf_op jit(solution)/shard_map/while/body/eval_jaxpr/ppermute | solution.py:25
  101.7 1.6 copy-start.8
  105.4 27.0 %collective-permute-start = (bf16[2,512,512]{1,0,2:T(2,128)(2,1)S(1)}, bf16[2,512,512]{1,0,2:T(2,128)(2,1)}, u32[]{:S(2)}, u32[]{:S(2)}) collective-permute-start(bf16[2,512,512]{1,0,2:T(2,128)(2,1)S(1)} %get-tuple-element.1083), channel_id=1, source_target_pairs={{0,8},{8,16},{16,24},{1,9},{9,17},{17,25},{2,10},{10,18},{18,26},{... | collective-permute-start | bytes 3145736 | tf_op jit(solution)/shard_map/while/body/eval_jaxpr/ppermute | solution.py:25
  139.0 36.8 %collective-permute-start = (bf16[2,512,512]{1,0,2:T(2,128)(2,1)S(1)}, bf16[2,512,512]{1,0,2:T(2,128)(2,1)}, u32[]{:S(2)}, u32[]{:S(2)}) collective-permute-start(bf16[2,512,512]{1,0,2:T(2,128)(2,1)S(1)} %get-tuple-element.1083), channel_id=1, source_target_pairs={{0,8},{8,16},{16,24},{1,9},{9,17},{17,25},{2,10},{10,18},{18,26},{... | collective-permute-start | bytes 3145736 | tf_op jit(solution)/shard_map/while/body/eval_jaxpr/ppermute | solution.py:25
  182.4 25.3 %collective-permute-start = (bf16[2,512,512]{1,0,2:T(2,128)(2,1)S(1)}, bf16[2,512,512]{1,0,2:T(2,128)(2,1)}, u32[]{:S(2)}, u32[]{:S(2)}) collective-permute-start(bf16[2,512,512]{1,0,2:T(2,128)(2,1)S(1)} %get-tuple-element.1083), channel_id=1, source_target_pairs={{0,8},{8,16},{16,24},{1,9},{9,17},{17,25},{2,10},{10,18},{18,26},{... | collective-permute-start | bytes 3145736 | tf_op jit(solution)/shard_map/while/body/eval_jaxpr/ppermute | solution.py:25
  214.3 33.6 %collective-permute-start = (bf16[2,512,512]{1,0,2:T(2,128)(2,1)S(1)}, bf16[2,512,512]{1,0,2:T(2,128)(2,1)}, u32[]{:S(2)}, u32[]{:S(2)}) collective-permute-start(bf16[2,512,512]{1,0,2:T(2,128)(2,1)S(1)} %get-tuple-element.1083), channel_id=1, source_target_pairs={{0,8},{8,16},{16,24},{1,9},{9,17},{17,25},{2,10},{10,18},{18,26},{... | collective-permute-start | bytes 3145736 | tf_op jit(solution)/shard_map/while/body/eval_jaxpr/ppermute | solution.py:25
  247.9 2.3 copy-start.9
  250.3 1.6 copy-start.2
  261.7 24.9 %collective-permute-start.1 = (bf16[2,512,512]{2,1,0:T(8,128)(2,1)}, bf16[2,512,512]{2,1,0:T(8,128)(2,1)}, u32[]{:S(2)}, u32[]{:S(2)}) collective-permute-start(bf16[2,512,512]{2,1,0:T(8,128)(2,1)} %get-tuple-element.963), channel_id=1, source_target_pairs={{8,0},{16,8},{24,16},{9,1},{17,9},{25,17},{10,2},{18,10},{26,18},{... | collective-permute-start | bytes 3145736 | tf_op jit(solution)/shard_map/while/body/eval_jaxpr/ppermute | solution.py:25
  263.0 3.4 copy-start.3
  264.5 2.9 copy-start
  266.6 2.9 copy-start.4
  269.5 17.1 %copy-start.1 = (f32[2,2,512,512]{3,2,1,0:T(8,128)}, f32[2,2,512,512]{3,2,1,0:T(8,128)S(1)}, u32[]{:S(2)}) copy-start(f32[2,2,512,512]{3,2,1,0:T(8,128)S(1)} %bitcast_dynamic-update-slice_fusion.6) | copy-start | bytes 12582916 | tf_op jit(solution)/shard_map/while
  289.4 33.8 %collective-permute-start.1 = (bf16[2,512,512]{2,1,0:T(8,128)(2,1)}, bf16[2,512,512]{2,1,0:T(8,128)(2,1)}, u32[]{:S(2)}, u32[]{:S(2)}) collective-permute-start(bf16[2,512,512]{2,1,0:T(8,128)(2,1)} %get-tuple-element.963), channel_id=1, source_target_pairs={{8,0},{16,8},{24,16},{9,1},{17,9},{25,17},{10,2},{18,10},{26,18},{... | collective-permute-start | bytes 3145736 | tf_op jit(solution)/shard_map/while/body/eval_jaxpr/ppermute | solution.py:25
  290.7 3.4 copy-start.3
  292.1 2.9 copy-start
  294.3 2.9 copy-start.4
  297.2 26.0 %copy-start.1 = (f32[2,2,512,512]{3,2,1,0:T(8,128)}, f32[2,2,512,512]{3,2,1,0:T(8,128)S(1)}, u32[]{:S(2)}) copy-start(f32[2,2,512,512]{3,2,1,0:T(8,128)S(1)} %bitcast_dynamic-update-slice_fusion.6) | copy-start | bytes 12582916 | tf_op jit(solution)/shard_map/while
  326.0 67.2 %collective-permute-start.1 = (bf16[2,512,512]{2,1,0:T(8,128)(2,1)}, bf16[2,512,512]{2,1,0:T(8,128)(2,1)}, u32[]{:S(2)}, u32[]{:S(2)}) collective-permute-start(bf16[2,512,512]{2,1,0:T(8,128)(2,1)} %get-tuple-element.963), channel_id=1, source_target_pairs={{8,0},{16,8},{24,16},{9,1},{17,9},{25,17},{10,2},{18,10},{26,18},{... | collective-permute-start | bytes 3145736 | tf_op jit(solution)/shard_map/while/body/eval_jaxpr/ppermute | solution.py:25
  327.3 3.4 copy-start.3
  328.8 2.9 copy-start
  330.9 2.9 copy-start.4
  333.8 59.3 %copy-start.1 = (f32[2,2,512,512]{3,2,1,0:T(8,128)}, f32[2,2,512,512]{3,2,1,0:T(8,128)S(1)}, u32[]{:S(2)}) copy-start(f32[2,2,512,512]{3,2,1,0:T(8,128)S(1)} %bitcast_dynamic-update-slice_fusion.6) | copy-start | bytes 12582916 | tf_op jit(solution)/shard_map/while
  410.7 22.6 %collective-permute-start.1 = (bf16[2,512,512]{2,1,0:T(8,128)(2,1)}, bf16[2,512,512]{2,1,0:T(8,128)(2,1)}, u32[]{:S(2)}, u32[]{:S(2)}) collective-permute-start(bf16[2,512,512]{2,1,0:T(8,128)(2,1)} %get-tuple-element.963), channel_id=1, source_target_pairs={{8,0},{16,8},{24,16},{9,1},{17,9},{25,17},{10,2},{18,10},{26,18},{... | collective-permute-start | bytes 3145736 | tf_op jit(solution)/shard_map/while/body/eval_jaxpr/ppermute | solution.py:25
  412.0 3.4 copy-start.3
  413.4 2.9 copy-start
  415.6 2.9 copy-start.4
  418.5 14.8 %copy-start.1 = (f32[2,2,512,512]{3,2,1,0:T(8,128)}, f32[2,2,512,512]{3,2,1,0:T(8,128)S(1)}, u32[]{:S(2)}) copy-start(f32[2,2,512,512]{3,2,1,0:T(8,128)S(1)} %bitcast_dynamic-update-slice_fusion.6) | copy-start | bytes 12582916 | tf_op jit(solution)/shard_map/while
  450.7 21.7 %collective-permute-start.1 = (bf16[2,512,512]{2,1,0:T(8,128)(2,1)}, bf16[2,512,512]{2,1,0:T(8,128)(2,1)}, u32[]{:S(2)}, u32[]{:S(2)}) collective-permute-start(bf16[2,512,512]{2,1,0:T(8,128)(2,1)} %get-tuple-element.963), channel_id=1, source_target_pairs={{8,0},{16,8},{24,16},{9,1},{17,9},{25,17},{10,2},{18,10},{26,18},{... | collective-permute-start | bytes 3145736 | tf_op jit(solution)/shard_map/while/body/eval_jaxpr/ppermute | solution.py:25
  452.0 3.4 copy-start.3
  453.5 2.9 copy-start
  455.6 2.9 copy-start.4
  458.6 13.9 %copy-start.1 = (f32[2,2,512,512]{3,2,1,0:T(8,128)}, f32[2,2,512,512]{3,2,1,0:T(8,128)S(1)}, u32[]{:S(2)}) copy-start(f32[2,2,512,512]{3,2,1,0:T(8,128)S(1)} %bitcast_dynamic-update-slice_fusion.6) | copy-start | bytes 12582916 | tf_op jit(solution)/shard_map/while
  479.8 17.8 %copy-start.5 = (f32[2,512,512]{2,1,0:T(8,128)S(1)}, f32[2,512,512]{2,1,0:T(8,128)}, u32[]{:S(2)}) copy-start(f32[2,512,512]{2,1,0:T(8,128)} %get-tuple-element.612) | copy-start | bytes 6291460
  528.2 2.1 collective-permute-start.4
  528.3 2.8 collective-permute-start.5
Sparse Core Ops, SparseCore 0:
  534.8 35.5 reduce-scatter.1
where the time goes:
time: 584 us; the launch traced here: 581 us
  waiting for transfers between devices  228 us (39%)
  local copies, waits for them, and re-layouts  163 us (28%)
  other arithmetic  90.7 us (16%)
  starting transfers between devices  51.4 us (9%)
  matrix products  25.1 us (4%)
  between operations  21.1 us (4%)
    ppermute x10, waiting for transfers between devices, passed_along(): return lax.ppermute(x, axis, pairs)  190 us
    ppermute x10, starting transfers between devices, passed_along(): return lax.ppermute(x, axis, pairs)  50.3 us
    dynamic_update_slice x2, local copies, waits for them, and re-layouts, shards(): lax.dynamic_update_slice(accum_grid, current_block + pieces[position], an...  39.6 us
    reduce_scatter x1, waiting for transfers between devices, shards(): lax.psum_scatter(folded.astype(jnp.bfloat16), 'probe', scatter_dimension=...  35.7 us
    broadcast_in_dim x5, other arithmetic, forward_tick(): lax.dynamic_update_index_in_dim(saved, jnp.where(valid, wave_in, previous...  18.7 us
    another operation x18, local copies, waits for them, and re-layouts  17 us
    dynamic_update_slice x10, local copies, waits for them, and re-layouts, forward_tick(): lax.dynamic_update_index_in_dim(finals, jnp.where(keep_final, produced, e...  14.8 us
    dynamic_update_slice x5, local copies, waits for them, and re-layouts, forward_tick(): lax.dynamic_update_index_in_dim(saved, jnp.where(valid, wave_in, previous...  12.2 us
  transfers between devices with their start and end apart: 15, of which 13 were waited for; matrix products, arithmetic and copies ran while one was open for 15% of the time, Pallas kernels for 0%

commit v1 on v0

v1 whole, which is shorter than its diff:
```python
import functools

import jax
import jax.numpy as jnp
from jax import lax
from jax.experimental import pallas as pl
from jax.experimental.pallas import tpu as pltpu
from jax.sharding import PartitionSpec as P

MARGIN = 128
F32 = jnp.float32
BF16 = jnp.bfloat16


def ring(count, by):
    return [(i, (i + by) % count) for i in range(count)]


def swapped(count, bit):
    return [(i, i ^ bit) for i in range(count)]


def spread(piece, bits):
    count = lax.axis_size("probe")
    held, order = piece[None], [0]
    for bit in bits:
        held = jnp.concatenate([held, lax.ppermute(held, "probe", swapped(count, bit))], axis=0)
        order = order + [j ^ bit for j in order]
    return held, order


def dot(a, b):
    return jnp.dot(a, b, preferred_element_type=F32)


CHUNK = 64
ALIGN = 16


def body(
    order_a,
    order_b,
    slice_count,
    info,
    starts,
    own,
    own_top,
    own_bottom,
    far_real,
    far_imag,
    far_top,
    far_bottom,
    probe,
    row_mat,
    row_mat_t,
    col_mat,
    col_mat_t,
    measured,
    out,
    stage,
    wins,
    saved,
    work,
    middle,
    wave,
    amplitude,
    probe_v,
    mats,
    grid,
    sem_stage,
    sem_mat,
    sem_in,
):
    size = probe_v.shape[1]
    count = wave.shape[0]
    own_rows = own.shape[1]
    lanes = size + 128
    mine, place = info[0], info[1]
    pieces = far_real.shape[1]
    piece_rows = own_rows // pieces
    col_last = (grid.shape[2] - size) // 128 - 1

    def stage_copies(k, act):
        slot = lax.rem(k, 2)
        sem = sem_stage.at[slot]

        def one(src, comp, first, rows):
            copy = pltpu.make_async_copy(src, stage.at[slot, comp, pl.ds(first, rows), :], sem)
            copy.start() if act else copy.wait()

        @pl.when(k == mine)
        def _():
            for comp in range(2):
                one(own_top.at[comp], comp, 0, MARGIN)
                one(own.at[comp], comp, MARGIN, own_rows)
                one(own_bottom.at[comp], comp, MARGIN + own_rows, MARGIN)

        @pl.when(k != mine)
        def _():
            far = lax.rem(mine - k + slice_count, slice_count) - 1
            for comp in range(2):
                source, order = ((far_real, order_a), (far_imag, order_b))[comp]
                one(far_top.at[far, comp], comp, 0, MARGIN)
                for j in range(pieces):
                    first = pl.multiple_of(MARGIN + (place ^ order[j]) * piece_rows, ALIGN)
                    one(source.at[far, j], comp, first, piece_rows)
                one(far_bottom.at[far, comp], comp, MARGIN + own_rows, MARGIN)

    mat_sources = (col_mat, row_mat, col_mat_t, row_mat_t)
    mat_copies = [
        pltpu.make_async_copy(source, mats.at[i], sem_mat.at[i])
        for i, source in enumerate(mat_sources)
    ]
    probe_copy = pltpu.make_async_copy(probe, probe_v, sem_in.at[0])
    measured_copy = pltpu.make_async_copy(measured, amplitude, sem_in.at[1])
    probe_copy.start()
    stage_copies(jnp.int32(0), True)
    for copy in mat_copies:
        copy.start()
    measured_copy.start()

    def clear(i, _):
        rows = pl.ds(pl.multiple_of(i * 8, 8), 8)
        for comp in range(3):
            grid[comp, rows, :] = jnp.zeros((8, grid.shape[2]), F32)
        return 0

    lax.fori_loop(0, grid.shape[1] // 8, clear, 0)
    probe_copy.wait()

    def fill(i, _):
        rows = pl.multiple_of(i * CHUNK, CHUNK)
        for comp in range(2):
            value = probe_v[comp, pl.ds(rows, CHUNK), :]
            for position in range(count):
                wave[position, pl.ds(rows + comp * size, CHUNK), :] = value
        return 0

    lax.fori_loop(0, size // CHUNK, fill, 0)

    def column(position):
        col = starts[position, 1]
        tile = jnp.minimum(col // 128, col_last)
        return pl.multiple_of(tile * 128, 128), col - tile * 128

    def add_piece(position, comp, i, value):
        row = starts[position, 0] + i * CHUNK
        inside = lax.rem(row, 8)
        first = pl.multiple_of(row - inside, 8)
        col_first, shift = column(position)
        wide = jnp.concatenate([value, jnp.zeros((CHUNK, 128), F32)], axis=1)
        wide = pltpu.roll(wide, shift, 1)
        tall = jnp.concatenate([wide, jnp.zeros((8, lanes), F32)], axis=0)
        tall = pltpu.roll(tall, inside, 0)
        grid[comp, pl.ds(first, CHUNK + 8), pl.ds(col_first, lanes)] += tall

    def halves(position, i):
        rows = pl.multiple_of(i * CHUNK, CHUNK)
        return (
            wave[position, pl.ds(rows, CHUNK), :].astype(F32),
            wave[position, pl.ds(rows + size, CHUNK), :].astype(F32),
        )

    def put_work(position, i, real, imag):
        rows = pl.ds(pl.multiple_of(i * CHUNK, CHUNK), CHUNK)
        work[position, rows, pl.ds(0, size)] = real.astype(BF16)
        work[position, rows, pl.ds(size, size)] = imag.astype(BF16)

    def propagate(position, col, row):
        for n in range(2):
            part = dot(work[position], mats[col, :, pl.ds(n * size, size)])
            middle[position, pl.ds(n * size, size), :] = part.astype(BF16)
        for m in range(2):
            part = dot(mats[row, pl.ds(m * size, size), :], middle[position])
            wave[position, pl.ds(m * size, size), :] = part.astype(BF16)

    def forward(k, _):
        slot = lax.rem(k, 2)
        stage_copies(k, False)

        @pl.when(k + 1 < slice_count)
        def _():
            stage_copies(k + 1, True)

        for position in range(count):
            row_start = starts[position, 0]
            col_first, shift = column(position)
            back_shift = lax.rem(lanes - shift, lanes)

            def enter(i, _):
                row = row_start + i * CHUNK
                inside = lax.rem(row, ALIGN)
                first = pl.multiple_of(row - inside, ALIGN)
                height = CHUNK + ALIGN

                def window(comp):
                    block = stage[
                        slot, comp, pl.ds(first, height), pl.ds(col_first, lanes)
                    ].astype(F32)
                    block = pltpu.roll(block, lax.rem(height - inside, height), 0)[:CHUNK]
                    return pltpu.roll(block, back_shift, 1)[:, :size]

                win_real, win_imag = window(0), window(1)
                rows = pl.ds(pl.multiple_of(i * CHUNK, CHUNK), CHUNK)
                wins[k, position, 0, rows, :] = win_real.astype(BF16)
                wins[k, position, 1, rows, :] = win_imag.astype(BF16)
                real, imag = halves(position, i)

                @pl.when(k == mine)
                def _():
                    saved[position, 0, rows, :] = real.astype(BF16)
                    saved[position, 1, rows, :] = imag.astype(BF16)
                    add_piece(position, 2, i, real * real + imag * imag)

                put_work(
                    position,
                    i,
                    real * win_real - imag * win_imag,
                    real * win_imag + imag * win_real,
                )
                return 0

            lax.fori_loop(0, size // CHUNK, enter, 0)

        @pl.when(k == 0)
        def _():
            mat_copies[0].wait()
            mat_copies[1].wait()

        for position in range(count):
            propagate(position, 0, 1)
        return 0

    lax.fori_loop(0, slice_count, forward, 0)
    measured_copy.wait()

    for position in range(count):

        def detect(i, _):
            real, imag = halves(position, i)
            seen = amplitude[position, pl.ds(pl.multiple_of(i * CHUNK, CHUNK), CHUNK), :]
            factor = 1.0 - seen / jnp.sqrt(real * real + imag * imag + 1.0)
            put_work(position, i, real * factor, imag * factor)
            return 0

        lax.fori_loop(0, size // CHUNK, detect, 0)

    mat_copies[2].wait()
    mat_copies[3].wait()

    def backward(step, _):
        k = slice_count - 1 - step
        for position in range(count):
            propagate(position, 2, 3)
        for position in range(count):

            def leave(i, _):
                rows = pl.ds(pl.multiple_of(i * CHUNK, CHUNK), CHUNK)
                real, imag = halves(position, i)

                @pl.when(k == mine)
                def _():
                    old_real = saved[position, 0, rows, :].astype(F32)
                    old_imag = saved[position, 1, rows, :].astype(F32)
                    add_piece(position, 0, i, old_real * real + old_imag * imag)
                    add_piece(position, 1, i, old_real * imag - old_imag * real)

                @pl.when(k != mine)
                def _():
                    win_real = wins[k, position, 0, rows, :].astype(F32)
                    win_imag = wins[k, position, 1, rows, :].astype(F32)
                    put_work(
                        position,
                        i,
                        win_real * real + win_imag * imag,
                        win_real * imag - win_imag * real,
                    )

                return 0

            lax.fori_loop(0, size // CHUNK, leave, 0)
        return 0

    lax.fori_loop(0, slice_count - mine, backward, 0)

    def emit(i, _):
        rows = pl.ds(pl.multiple_of(i * 16, 16), 16)
        for comp in range(3):
            out[comp, rows, :] = grid[comp, rows, :].astype(BF16)
        return 0

    lax.fori_loop(0, out.shape[1] // 16, emit, 0)


def swap_margins(x, dim):
    count, length = (lax.axis_size("tile"), x.shape[dim])
    last = lax.slice_in_dim(x, length - MARGIN, length, axis=dim)
    leading = lax.slice_in_dim(x, 0, MARGIN, axis=dim)
    before = lax.ppermute(last, "tile", ring(count, 1))
    after = lax.ppermute(leading, "tile", ring(count, -1))
    return before, after


def rows_of(held, order, place, first, stop, piece_rows):
    picked = []
    lookup = jnp.array([order.index(j) for j in range(len(order))], jnp.int32)
    for piece in range(first // piece_rows, stop // piece_rows):
        picked.append(lax.dynamic_index_in_dim(held, lookup[piece ^ place], 0, keepdims=False))
    return jnp.concatenate(picked, axis=-2)


def shards(probe_wave, fresnel_rows, fresnel_cols, object_slices, offsets, measured):
    cut_count = lax.axis_size("cuts")
    probe_count = lax.axis_size("probe")
    section = lax.axis_index("cuts")
    place = lax.axis_index("probe")
    owned = object_slices[0]
    own_count = owned.shape[1]
    width_cols = owned.shape[2]
    size = probe_wave.shape[1]
    count = offsets.shape[1]
    piece_rows = own_count // probe_count
    bits = [1 << b for b in range(probe_count.bit_length() - 1)]

    own = owned.astype(BF16)
    own_top, own_bottom = swap_margins(own, 1)
    piece = lax.dynamic_slice_in_dim(own, place * piece_rows, piece_rows, axis=1)

    reals, imags, tops, bottoms = [], [], [], []
    for _ in range(cut_count - 1):
        piece = lax.ppermute(piece, "cuts", ring(cut_count, 1))
        real, order_a = spread(piece[0], bits)
        imag, order_b = spread(piece[1], bits[::-1])
        last = [
            rows_of(h, o, place, own_count - MARGIN, own_count, piece_rows)
            for h, o in ((real, order_a), (imag, order_b))
        ]
        lead = [
            rows_of(h, o, place, 0, MARGIN, piece_rows)
            for h, o in ((real, order_a), (imag, order_b))
        ]
        tiles = lax.axis_size("tile")
        tops.append(lax.ppermute(jnp.stack(last), "tile", ring(tiles, 1)))
        bottoms.append(lax.ppermute(jnp.stack(lead), "tile", ring(tiles, -1)))
        reals.append(real)
        imags.append(imag)

    row_real, row_imag = (fresnel_rows[0], fresnel_rows[1])
    col_real, col_imag = (fresnel_cols[0], fresnel_cols[1])
    row_mat = jnp.concatenate(
        [
            jnp.concatenate([row_real, -row_imag], axis=1),
            jnp.concatenate([row_imag, row_real], axis=1),
        ],
        axis=0,
    )
    col_mat_t = jnp.concatenate(
        [
            jnp.concatenate([col_real, -col_imag], axis=1),
            jnp.concatenate([col_imag, col_real], axis=1),
        ],
        axis=0,
    )

    info = jnp.stack([section, place]).astype(jnp.int32)
    anywhere = pl.BlockSpec(memory_space=pl.ANY)
    scalars = pl.BlockSpec(memory_space=pltpu.SMEM)
    tall = own_count + 2 * MARGIN
    grid = pl.pallas_call(
        functools.partial(body, tuple(order_a), tuple(order_b), cut_count),
        out_shape=jax.ShapeDtypeStruct((3, tall, width_cols), BF16),
        in_specs=[scalars, scalars] + [anywhere] * 13,
        out_specs=pl.BlockSpec(memory_space=pltpu.VMEM),
        scratch_shapes=[
            pltpu.VMEM((2, 2, tall + ALIGN, width_cols), BF16),
            pltpu.VMEM((cut_count, count, 2, size, size), BF16),
            pltpu.VMEM((count, 2, size, size), BF16),
            pltpu.VMEM((count, size, 2 * size), BF16),
            pltpu.VMEM((count, 2 * size, size), BF16),
            pltpu.VMEM((count, 2 * size, size), BF16),
            pltpu.VMEM((count, size, size), F32),
            pltpu.VMEM((2, size, size), BF16),
            pltpu.VMEM((4, 2 * size, 2 * size), BF16),
            pltpu.VMEM((3, tall + 8, width_cols), F32),
            pltpu.SemaphoreType.DMA((2,)),
            pltpu.SemaphoreType.DMA((4,)),
            pltpu.SemaphoreType.DMA((2,)),
        ],
        compiler_params=pltpu.CompilerParams(vmem_limit_bytes=62 * 1024 * 1024),
        name="gradient",
    )(
        info,
        offsets[0],
        own,
        own_top,
        own_bottom,
        jnp.stack(reals),
        jnp.stack(imags),
        jnp.stack(tops),
        jnp.stack(bottoms),
        probe_wave,
        row_mat,
        row_mat.T,
        col_mat_t.T,
        col_mat_t,
        measured[0],
    )

    tiles = lax.axis_size("tile")
    inside = grid[:, MARGIN : MARGIN + own_count]
    upper = lax.ppermute(grid[:, MARGIN + own_count :], "tile", ring(tiles, 1))
    lower = lax.ppermute(grid[:, :MARGIN], "tile", ring(tiles, -1))
    folded = jnp.concatenate(
        [
            inside[:, :MARGIN].astype(F32) + upper.astype(F32),
            inside[:, MARGIN : own_count - MARGIN].astype(F32),
            inside[:, own_count - MARGIN :].astype(F32) + lower.astype(F32),
        ],
        axis=1,
    ).astype(BF16)

    def rows_for(index):
        return lax.dynamic_slice_in_dim(folded, index * piece_rows, piece_rows, axis=1)

    summed = rows_for(place).astype(F32)
    for j in range(1, probe_count):
        arrived = lax.ppermute(rows_for(place ^ j), "probe", swapped(probe_count, j))
        summed = summed + arrived.astype(F32)
    own_part = lax.dynamic_slice_in_dim(owned, place * piece_rows, piece_rows, 1)
    updated = own_part - summed[:2] / (summed[2] + 1.0)
    return updated[None]


def solution(mesh):
    in_specs = (
        P(),
        P(),
        P(),
        P("cuts", None, "tile", None),
        P("tile", "probe", None),
        P("tile", "probe", None, None),
    )
    out_specs = P("cuts", None, ("tile", "probe"), None)
    return jax.shard_map(shards, mesh=mesh, in_specs=in_specs, out_specs=out_specs, check_vma=False)
```

time: 584 us -> 212 us (0.36)
  waiting for transfers between devices: 228 us -> 64.4 us
  local copies, waits for them, and re-layouts: 163 us -> 19.4 us
  Pallas kernels: 0 us -> 70.9 us
  other arithmetic: 90.7 us -> 29.9 us
  starting transfers between devices: 51.4 us -> 22.7 us
  matrix products: 25.1 us -> 0 us
  between operations: 21.1 us -> 3.92 us
    ppermute x14 -> x28, waiting for transfers between devices: 193 us -> 64.4 us  [the longest x3 26 us: shards(): lax.ppermute(rows_for(place ^ j), 'probe', swapped(probe_count, j))]
    pallas_call x0 -> x1, Pallas kernels: none -> 70.9 us  [shards(): pl.pallas_call(functools.partial(body, tuple(order_a), tuple(order_b), cu...]
    dynamic_update_slice x17 -> x0, local copies, waits for them, and re-layouts: 66.6 us -> none  [the longest x2 39.6 us: shards(): lax.dynamic_update_slice(accum_grid, current_block + pieces[position], an...]
    reduce_scatter x1 -> x0, waiting for transfers between devices: 35.7 us -> none  [shards(): lax.psum_scatter(folded.astype(jnp.bfloat16), 'probe', scatter_dimension=...]
    dynamic_slice x30 -> x6, local copies, waits for them, and re-layouts: 39.6 us -> 4.01 us  [the longest x3 2.25 us: rows_of(): lax.dynamic_index_in_dim(held, lookup[piece ^ place], 0, keepdims=False)]
    ppermute x14 -> x28, starting transfers between devices: 51.4 us -> 22.7 us  [the longest x12 13.8 us: spread(): lax.ppermute(held, 'probe', swapped(count, bit))]
    dot_general x12 -> x0, matrix products: 25.1 us -> none  [the longest x2 8.44 us: adjoint_apply(): result = jnp.dot(left_block, middle, preferred_element_type=jnp.float32)]
    broadcast_in_dim x10 -> x0, other arithmetic: 24.1 us -> none  [the longest x5 18.7 us: forward_tick(): lax.dynamic_update_index_in_dim(saved, jnp.where(valid, wave_in, previous...]
  transfers between devices with their start and end apart: 15 -> 28, of which waited for: 13 -> 15; matrix products, arithmetic and copies ran while one was open for 15% -> 17% of each run, Pallas kernels for 0% -> 0%
where the time goes in v1:
time: 212 us; the launch traced here: 211 us
  Pallas kernels  70.9 us (33%)
  waiting for transfers between devices  64.4 us (30%)
  other arithmetic  29.9 us (14%)
  starting transfers between devices  22.7 us (11%)
  local copies, waits for them, and re-layouts  19.4 us (9%)
  between operations  3.92 us (2%)
    pallas_call x1, Pallas kernels, shards(): pl.pallas_call(functools.partial(body, tuple(order_a), tuple(order_b), cu...  70.9 us
    ppermute x3, waiting for transfers between devices, shards(): lax.ppermute(rows_for(place ^ j), 'probe', swapped(probe_count, j))  26 us
    ppermute x12, waiting for transfers between devices, spread(): lax.ppermute(held, 'probe', swapped(count, bit))  25.1 us
    ppermute x12, starting transfers between devices, spread(): lax.ppermute(held, 'probe', swapped(count, bit))  13.8 us
    ppermute x3, waiting for transfers between devices, shards(): piece = lax.ppermute(piece, 'cuts', ring(cut_count, 1))  10.6 us
    concatenate x12, other arithmetic, spread(): jnp.concatenate([held, lax.ppermute(held, 'probe', swapped(count, bit))],...  7.38 us
  transfers between devices with their start and end apart: 28, of which 15 were waited for; matrix products, arithmetic and copies ran while one was open for 17% of the time, Pallas kernels for 0%

profile of v1, /device:TPU:0, one launch (start us, length us, event | category | flops | bytes accessed | tf_op | source)
XLA Modules:
  0.0 211.2 jit_solution(5521937670415103473)
XLA Ops:
  0.0 3.4 %convert_element_type.31 = bf16[1,2,512,768]{3,2,1,0:T(8,128)(2,1)} convert(f32[1,2,512,768]{3,2,1,0:T(8,128)} %param.21) | non-fusion elementwise | flops 786432 | bytes 4718592 | tf_op jit(solution)/shard_map/convert_element_type | solution.py:325
  3.4 1.0 dynamic-slice_bitcast_fusion
  4.4 3.1 %collective-permute-start.2 = (bf16[2,128,768]{2,1,0:T(8,128)(2,1)S(1)}, bf16[2,128,768]{2,1,0:T(8,128)(2,1)}, u32[]{:S(2)}, u32[]{:S(2)}) collective-permute-start(bf16[2,128,768]{2,1,0:T(8,128)(2,1)S(1)} %dynamic-slice_bitcast_fusion), channel_id=1, source_target_pairs={{0,8},{8,16},{16,24},{24,0},{1,9},{9,17},{17,25},{25,1},{2,10},{10... | collective-permute-start | bytes 1179656 | tf_op jit(solution)/shard_map/ppermute | solution.py:331
  7.7 1.2 copy-done.2
  8.9 1.0 fusion.13
  10.2 1.0 copy.23
  11.3 7.4 %collective-permute-done.2 = bf16[2,128,768]{2,1,0:T(8,128)(2,1)} collective-permute-done((bf16[2,128,768]{2,1,0:T(8,128)(2,1)S(1)}, bf16[2,128,768]{2,1,0:T(8,128)(2,1)}, u32[]{:S(2)}, u32[]{:S(2)}) %collective-permute-start.2) | collective-permute-done | bytes 393248 | tf_op jit(solution)/shard_map/ppermute | solution.py:331
  18.8 1.0 fusion.15
  19.8 1.6 collective-permute-start.3
  21.4 1.9 fusion.11
  23.3 1.5 collective-permute-start.11
  24.8 1.2 collective-permute-done.3
  26.0 0.9 pad_maximum_fusion.11
  26.8 1.3 collective-permute-start.4
  28.1 2.9 %collective-permute-done.5 = bf16[2,128,768]{2,1,0:T(8,128)(2,1)S(1)} collective-permute-done((bf16[2,128,768]{2,1,0:T(8,128)(2,1)}, bf16[2,128,768]{2,1,0:T(8,128)(2,1)S(1)}, u32[]{:S(2)}, u32[]{:S(2)}) %collective-permute-start.5) | collective-permute-done | bytes 393248 | tf_op jit(solution)/shard_map/ppermute | solution.py:331
  31.8 1.3 collective-permute-start.13
  33.1 2.6 %maximum_maximum_fusion.1 = (bf16[1024,1024]{1,0:T(8,128)(2,1)}, bf16[1024,1024]{0,1:T(8,128)(2,1)}) fusion(bf16[512,512]{1,0:T(8,128)(2,1)S(1)} %get-tuple-element.19, bf16[512,512]{1,0:T(8,128)(2,1)S(1)} %get-tuple-element.18, bf16[512,512]{1,0:T(8,128)(2,1)S(1)} %fusion.3), kind=kLoop, calls=%fused_computation.4 | loop fusion | flops 8388608 | bytes 5767168 | tf_op jit(solution)/shard_map/concatenate | solution.py:357
  39.8 1.6 collective-permute-start.6
  42.3 5.4 %collective-permute-done.6 = bf16[1,128,768]{2,1,0:T(8,128)(2,1)S(1)} collective-permute-done((bf16[1,128,768]{2,1,0:T(8,128)(2,1)S(1)}, bf16[1,128,768]{2,1,0:T(8,128)(2,1)S(1)}, u32[]{:S(2)}, u32[]{:S(2)}) %collective-permute-start.6) | collective-permute-done | bytes 196640 | tf_op jit(solution)/shard_map/ppermute | solution.py:27
  47.7 1.5 collective-permute-start.14
  50.5 1.3 pad_maximum_fusion.5
  52.1 1.4 collective-permute-start.15
  53.4 2.7 %collective-permute-done.12 = bf16[2,128,768]{2,1,0:T(8,128)(2,1)S(1)} collective-permute-done((bf16[2,128,768]{2,1,0:T(8,128)(2,1)S(1)}, bf16[2,128,768]{2,1,0:T(8,128)(2,1)S(1)}, u32[]{:S(2)}, u32[]{:S(2)}) %collective-permute-start.12) | collective-permute-done | bytes 393248 | tf_op jit(solution)/shard_map/ppermute | solution.py:27
  56.1 1.0 pad_maximum_fusion.8
  57.9 1.5 collective-permute-start.9
  61.4 7.4 %collective-permute-done.9 = bf16[1,128,768]{2,1,0:T(8,128)(2,1)S(1)} collective-permute-done((bf16[1,128,768]{2,1,0:T(8,128)(2,1)S(1)}, bf16[1,128,768]{2,1,0:T(8,128)(2,1)S(1)}, u32[]{:S(2)}, u32[]{:S(2)}) %collective-permute-start.9) | collective-permute-done | bytes 196640 | tf_op jit(solution)/shard_map/ppermute | solution.py:27
  69.4 1.0 pad_maximum_fusion.9
  70.9 1.0 pad_maximum_fusion.6
  71.9 2.4 %collective-permute-done.16 = bf16[2,128,768]{2,1,0:T(8,128)(2,1)S(1)} collective-permute-done((bf16[2,128,768]{2,1,0:T(8,128)(2,1)S(1)}, bf16[2,128,768]{2,1,0:T(8,128)(2,1)S(1)}, u32[]{:S(2)}, u32[]{:S(2)}) %collective-permute-start.16) | collective-permute-done | bytes 393248 | tf_op jit(solution)/shard_map/ppermute | solution.py:27
  74.3 1.0 pad_maximum_fusion.10
  76.0 5.4 %collective-permute-done.10 = bf16[2,128,768]{2,1,0:T(8,128)(2,1)S(1)} collective-permute-done((bf16[2,128,768]{2,1,0:T(8,128)(2,1)S(1)}, bf16[2,128,768]{2,1,0:T(8,128)(2,1)S(1)}, u32[]{:S(2)}, u32[]{:S(2)}) %collective-permute-start.10) | collective-permute-done | bytes 393248 | tf_op jit(solution)/shard_map/ppermute | solution.py:27
  81.4 1.0 pad_maximum_fusion.7
  85.9 2.6 %copy.21.row_mat = bf16[1024,1024]{1,0:T(8,128)(2,1)} copy(bf16[1024,1024]{0,1:T(8,128)(2,1)S(1)} %get-tuple-element.15) | data formatting | bytes 4194304 | tf_op jit(solution)/shard_map/concatenate | solution.py:350
  88.5 4.1 %copy.22.col_mat = bf16[1024,1024]{1,0:T(8,128)(2,1)} copy(bf16[1024,1024]{0,1:T(8,128)(2,1)} %get-tuple-element.13) | data formatting | bytes 4194304 | tf_op jit(solution)/shard_map/transpose | solution.py:404
  92.7 1.1 pad_maximum_fusion.18
  94.6 2.5 %pad_maximum_fusion = (bf16[3,4,128,768]{3,2,1,0:T(8,128)(2,1)}, bf16[3,4,128,768]{3,2,1,0:T(8,128)(2,1)}) fusion(bf16[1,4,128,768]{3,2,1,0:T(8,128)(2,1)S(1)} %copy-done.7, bf16[1,4,128,768]{3,2,1,0:T(8,128)(2,1)S(1)} %copy-done.5, bf16[1,4,128,768]{3,2,1,0:T(8,128)(2,1)S(1)} %get-tuple-element.35, bf16[1,4,128,768]{3,2,1,0:T(8,128)(2,1)S(1)} %copy-done.6, ...), kind=kLoop, calls=%fused_computation | loop fusion | flops 4718592 | bytes 9437184 | tf_op jit(solution)/shard_map/stack | solution.py:397
  97.0 2.5 %pad_maximum_fusion.4.far_bottom = bf16[3,2,128,768]{3,2,1,0:T(8,128)(2,1)} fusion(bf16[1,2,128,768]{3,2,1,0:T(8,128)(2,1)} %bitcast.19, bf16[1,2,128,768]{3,2,1,0:T(8,128)(2,1)} %bitcast.18, bf16[1,2,128,768]{3,2,1,0:T(8,128)(2,1)} %bitcast.17), kind=kLoop, calls=%fused_computation.6 | loop fusion | flops 1179648 | bytes 2359296 | tf_op jit(solution)/shard_map/stack | solution.py:400
  99.5 1.2 pad_maximum_fusion.3.far_top
  100.7 70.9 %gradient.1 = bf16[3,768,768]{2,1,0:T(8,128)(2,1)} custom-call(s32[2]{0:T(128)} %pad_add_fusion.info, s32[2,2]{1,0:T(2,128)} %bitcast.53, bf16[2,512,768]{2,1,0:T(8,128)(2,1)} %copy-done.2, bf16[2,128,768]{2,1,0:T(8,128)(2,1)} %collective-permute-done.own_top, bf16[2,128,768]{2,1,0:T(8,128)(2,1)} %collective-permute-done.1.own_bottom, ...), custom_call_target="tpu_custom_call" | custom-call | tf_op jit(solution)/shard_map/gradient/pallas_call | solution.py:369
  171.6 2.5 %fusion.12 = (bf16[3,128,768]{2,1,0:T(8,128)(2,1)}, bf16[3,128,768]{2,1,0:T(8,128)(2,1)}) fusion(bf16[3,768,768]{2,1,0:T(8,128)(2,1)} %gradient.1), kind=kLoop, calls=%fused_computation.62 | loop fusion | bytes 2359296 | tf_op jit(solution)/shard_map/slice | solution.py:411
  174.6 1.9 collective-permute-done.23
  176.5 0.8 collective-permute-done.24
  177.3 1.5 add_convert_fusion.1
  179.2 1.5 collective-permute-start.25
  181.2 1.5 collective-permute-start.27
  182.7 12.7 %collective-permute-done.25 = bf16[3,128,768]{2,1,0:T(8,128)(2,1)S(1)} collective-permute-done((bf16[3,128,768]{2,1,0:T(8,128)(2,1)S(1)}, bf16[3,128,768]{2,1,0:T(8,128)(2,1)S(1)}, u32[]{:S(2)}, u32[]{:S(2)}) %collective-permute-start.25) | collective-permute-done | bytes 589856 | tf_op jit(solution)/shard_map/ppermute | solution.py:427
  195.4 13.2 %collective-permute-done.26 = bf16[3,128,768]{2,1,0:T(8,128)(2,1)S(1)} collective-permute-done((bf16[3,128,768]{2,1,0:T(8,128)(2,1)S(1)}, bf16[3,128,768]{2,1,0:T(8,128)(2,1)S(1)}, u32[]{:S(2)}, u32[]{:S(2)}) %collective-permute-start.26) | collective-permute-done | bytes 589856 | tf_op jit(solution)/shard_map/ppermute | solution.py:427
  209.0 2.1 %fusion.1 = f32[1,2,128,768]{3,2,1,0:T(8,128)} fusion(f32[3,128,768]{2,1,0:T(8,128)S(1)} %convert_add_fusion, f32[1,2,512,768]{3,2,1,0:T(8,128)} %param.21, s32[]{:T(128)S(6)} %select_n.67, f32[128,768]{1,0:T(8,128)S(1)} %fusion.2), kind=kLoop, calls=%fused_computation.12 | loop fusion | flops 393216 | bytes 2752516 | tf_op jit(solution)/shard_map/broadcast_in_dim | solution.py:431
  (107 shorter events, 15.0 us)
Async XLA Ops:
  0.0 7.5 %copy-start = (f32[1,2,512,768]{3,2,1,0:T(8,128)S(1)}, f32[1,2,512,768]{3,2,1,0:T(8,128)}, u32[]{:S(2)}) copy-start(f32[1,2,512,768]{3,2,1,0:T(8,128)} %param.21) | copy-start | bytes 9437188
  4.4 5.4 %copy-start.11 = (bf16[2,512,512]{2,1,0:T(8,128)(2,1)S(1)}, bf16[2,512,512]{2,1,0:T(8,128)(2,1)}, u32[]{:S(2)}) copy-start(bf16[2,512,512]{2,1,0:T(8,128)(2,1)} %param.19) | copy-start | bytes 3145732
  4.4 14.4 %collective-permute-start.2 = (bf16[2,128,768]{2,1,0:T(8,128)(2,1)S(1)}, bf16[2,128,768]{2,1,0:T(8,128)(2,1)}, u32[]{:S(2)}, u32[]{:S(2)}) collective-permute-start(bf16[2,128,768]{2,1,0:T(8,128)(2,1)S(1)} %dynamic-slice_bitcast_fusion), channel_id=1, source_target_pairs={{0,8},{8,16},{16,24},{24,0},{1,9},{9,17},{17,25},{25,1},{2,10},{10... | collective-permute-start | bytes 1179656 | tf_op jit(solution)/shard_map/ppermute | solution.py:331
  9.8 90.8 %collective-permute-start = (bf16[2,128,768]{2,1,0:T(8,128)(2,1)}, bf16[2,128,768]{2,1,0:T(8,128)(2,1)}, u32[]{:S(2)}, u32[]{:S(2)}) collective-permute-start(bf16[2,128,768]{2,1,0:T(8,128)(2,1)} %get-tuple-element.17), channel_id=1, source_target_pairs={{0,4},{4,0},{1,5},{5,1},{2,6},{6,2},{3,7},{7,3},{8,12},{12,8},{9,1... | collective-permute-start | bytes 1179656 | tf_op jit(solution)/shard_map/ppermute | solution.py:299
  11.2 10.2 %copy-start.9 = (bf16[1,512,512]{1,2,0:T(8,128)(2,1)S(1)}, bf16[1,512,512]{1,2,0:T(8,128)(2,1)}, u32[]{:S(2)}) copy-start(bf16[1,512,512]{1,2,0:T(8,128)(2,1)} %copy.23) | copy-start | bytes 1572868
  18.8 12.3 %collective-permute-start.5 = (bf16[2,128,768]{2,1,0:T(8,128)(2,1)}, bf16[2,128,768]{2,1,0:T(8,128)(2,1)S(1)}, u32[]{:S(2)}, u32[]{:S(2)}) collective-permute-start(bf16[2,128,768]{2,1,0:T(8,128)(2,1)} %collective-permute-done.2), channel_id=1, source_target_pairs={{0,8},{8,16},{16,24},{24,0},{1,9},{9,17},{17,25},{25,1},{2,10},{10... | collective-permute-start | bytes 1179656 | tf_op jit(solution)/shard_map/ppermute | solution.py:331
  19.8 6.1 %copy-start.10 = (bf16[1,128,768]{2,1,0:T(8,128)(2,1)}, bf16[1,128,768]{2,1,0:T(8,128)(2,1)S(1)}, u32[]{:S(2)}) copy-start(bf16[1,128,768]{2,1,0:T(8,128)(2,1)S(1)} %get-tuple-element.47) | copy-start | bytes 589828
  19.8 6.1 %collective-permute-start.3 = (bf16[1,128,768]{2,1,0:T(8,128)(2,1)S(1)}, bf16[1,128,768]{2,1,0:T(8,128)(2,1)S(1)}, u32[]{:S(2)}, u32[]{:S(2)}) collective-permute-start(bf16[1,128,768]{2,1,0:T(8,128)(2,1)S(1)} %get-tuple-element.47), channel_id=1, source_target_pairs={{0,1},{1,0},{2,3},{3,2},{4,5},{5,4},{6,7},{7,6},{8,9},{9,8},{10,11... | collective-permute-start | bytes 589832 | tf_op jit(solution)/shard_map/ppermute | solution.py:27
  23.3 18.1 %collective-permute-start.11 = (bf16[1,128,768]{2,1,0:T(8,128)(2,1)S(1)}, bf16[1,128,768]{2,1,0:T(8,128)(2,1)S(1)}, u32[]{:S(2)}, u32[]{:S(2)}) collective-permute-start(bf16[1,128,768]{2,1,0:T(8,128)(2,1)S(1)} %get-tuple-element.46), channel_id=1, source_target_pairs={{0,2},{1,3},{2,0},{3,1},{4,6},{5,7},{6,4},{7,5},{8,10},{9,11},{10,... | collective-permute-start | bytes 589832 | tf_op jit(solution)/shard_map/ppermute | solution.py:27
  26.0 5.1 %copy-start.16 = (bf16[1,128,768]{2,1,0:T(8,128)(2,1)}, bf16[1,128,768]{2,1,0:T(8,128)(2,1)S(1)}, u32[]{:S(2)}) copy-start(bf16[1,128,768]{2,1,0:T(8,128)(2,1)S(1)} %collective-permute-done.3) | copy-start | bytes 589828
  26.8 22.4 %collective-permute-start.4 = (bf16[2,128,768]{2,1,0:T(8,128)(2,1)}, bf16[2,128,768]{2,1,0:T(8,128)(2,1)S(1)}, u32[]{:S(2)}, u32[]{:S(2)}) collective-permute-start(bf16[2,128,768]{2,1,0:T(8,128)(2,1)} %pad_maximum_fusion.11), channel_id=1, source_target_pairs={{0,2},{1,3},{2,0},{3,1},{4,6},{5,7},{6,4},{7,5},{8,10},{9,11},{10,... | collective-permute-start | bytes 1179656 | tf_op jit(solution)/shard_map/ppermute | solution.py:27
  31.8 9.8 %collective-permute-start.13 = (bf16[1,128,768]{2,1,0:T(8,128)(2,1)S(1)}, bf16[1,128,768]{2,1,0:T(8,128)(2,1)S(1)}, u32[]{:S(2)}, u32[]{:S(2)}) collective-permute-start(bf16[1,128,768]{2,1,0:T(8,128)(2,1)S(1)} %get-tuple-element.48), channel_id=1, source_target_pairs={{0,2},{1,3},{2,0},{3,1},{4,6},{5,7},{6,4},{7,5},{8,10},{9,11},{10,... | collective-permute-start | bytes 589832 | tf_op jit(solution)/shard_map/ppermute | solution.py:27
  33.1 2.6 %copy-start.22 = (s32[4]{0:T(128)S(1)}, s32[4]{0:T(128)}, u32[]{:S(2)}) copy-start(s32[4]{0:T(128)} %constant.55.clone) | copy-start | bytes 52
  39.8 7.8 %collective-permute-start.6 = (bf16[1,128,768]{2,1,0:T(8,128)(2,1)S(1)}, bf16[1,128,768]{2,1,0:T(8,128)(2,1)S(1)}, u32[]{:S(2)}, u32[]{:S(2)}) collective-permute-start(bf16[1,128,768]{2,1,0:T(8,128)(2,1)S(1)} %get-tuple-element.49), channel_id=1, source_target_pairs={{0,1},{1,0},{2,3},{3,2},{4,5},{5,4},{6,7},{7,6},{8,9},{9,8},{10,11... | collective-permute-start | bytes 589832 | tf_op jit(solution)/shard_map/ppermute | solution.py:27
  41.4 7.8 %copy-start.14 = (bf16[1,128,768]{2,1,0:T(8,128)(2,1)}, bf16[1,128,768]{2,1,0:T(8,128)(2,1)S(1)}, u32[]{:S(2)}) copy-start(bf16[1,128,768]{2,1,0:T(8,128)(2,1)S(1)} %collective-permute-done.11) | copy-start | bytes 589828
  41.4 10.7 %collective-permute-start.8 = (bf16[2,128,768]{2,1,0:T(8,128)(2,1)}, bf16[2,128,768]{2,1,0:T(8,128)(2,1)S(1)}, u32[]{:S(2)}, u32[]{:S(2)}) collective-permute-start(bf16[2,128,768]{2,1,0:T(8,128)(2,1)} %copy-done.21), channel_id=1, source_target_pairs={{0,8},{8,16},{16,24},{24,0},{1,9},{9,17},{17,25},{25,1},{2,10},{10... | collective-permute-start | bytes 1179656 | tf_op jit(solution)/shard_map/ppermute | solution.py:331
  41.6 7.6 %copy-start.12 = (bf16[1,128,768]{2,1,0:T(8,128)(2,1)}, bf16[1,128,768]{2,1,0:T(8,128)(2,1)S(1)}, u32[]{:S(2)}) copy-start(bf16[1,128,768]{2,1,0:T(8,128)(2,1)S(1)} %collective-permute-done.13) | copy-start | bytes 589828
  41.6 14.5 %collective-permute-start.12 = (bf16[2,128,768]{2,1,0:T(8,128)(2,1)S(1)}, bf16[2,128,768]{2,1,0:T(8,128)(2,1)S(1)}, u32[]{:S(2)}, u32[]{:S(2)}) collective-permute-start(bf16[2,128,768]{2,1,0:T(8,128)(2,1)S(1)} %pad_maximum_fusion.14), channel_id=1, source_target_pairs={{0,1},{1,0},{2,3},{3,2},{4,5},{5,4},{6,7},{7,6},{8,9},{9,8},{10,11... | collective-permute-start | bytes 1179656 | tf_op jit(solution)/shard_map/ppermute | solution.py:27
  47.7 21.1 %collective-permute-start.14 = (bf16[2,128,768]{2,1,0:T(8,128)(2,1)S(1)}, bf16[2,128,768]{2,1,0:T(8,128)(2,1)S(1)}, u32[]{:S(2)}, u32[]{:S(2)}) collective-permute-start(bf16[2,128,768]{2,1,0:T(8,128)(2,1)S(1)} %pad_maximum_fusion.15), channel_id=1, source_target_pairs={{0,1},{1,0},{2,3},{3,2},{4,5},{5,4},{6,7},{7,6},{8,9},{9,8},{10,11... | collective-permute-start | bytes 1179656 | tf_op jit(solution)/shard_map/ppermute | solution.py:27
  50.0 20.4 %collective-permute-start.7 = (bf16[2,128,768]{2,1,0:T(8,128)(2,1)S(1)}, bf16[2,128,768]{2,1,0:T(8,128)(2,1)S(1)}, u32[]{:S(2)}, u32[]{:S(2)}) collective-permute-start(bf16[2,128,768]{2,1,0:T(8,128)(2,1)S(1)} %pad_maximum_fusion.12), channel_id=1, source_target_pairs={{0,2},{1,3},{2,0},{3,1},{4,6},{5,7},{6,4},{7,5},{8,10},{9,11},{10,... | collective-permute-start | bytes 1179656 | tf_op jit(solution)/shard_map/ppermute | solution.py:27
  50.5 5.6 %copy-start.15 = (bf16[1,128,768]{2,1,0:T(8,128)(2,1)S(1)}, bf16[1,128,768]{2,1,0:T(8,128)(2,1)}, u32[]{:S(2)}) copy-start(bf16[1,128,768]{2,1,0:T(8,128)(2,1)} %copy-done.14) | copy-start | bytes 589828
  52.1 7.9 %collective-permute-start.15 = (bf16[1,128,768]{2,1,0:T(8,128)(2,1)S(1)}, bf16[1,128,768]{2,1,0:T(8,128)(2,1)S(1)}, u32[]{:S(2)}, u32[]{:S(2)}) collective-permute-start(bf16[1,128,768]{2,1,0:T(8,128)(2,1)S(1)} %get-tuple-element.50), channel_id=1, source_target_pairs={{0,2},{1,3},{2,0},{3,1},{4,6},{5,7},{6,4},{7,5},{8,10},{9,11},{10,... | collective-permute-start | bytes 589832 | tf_op jit(solution)/shard_map/ppermute | solution.py:27
  57.1 12.2 %copy-start.13 = (bf16[1,128,768]{2,1,0:T(8,128)(2,1)S(1)}, bf16[1,128,768]{2,1,0:T(8,128)(2,1)}, u32[]{:S(2)}) copy-start(bf16[1,128,768]{2,1,0:T(8,128)(2,1)} %copy-done.12) | copy-start | bytes 589828
  57.9 10.9 %collective-permute-start.9 = (bf16[1,128,768]{2,1,0:T(8,128)(2,1)S(1)}, bf16[1,128,768]{2,1,0:T(8,128)(2,1)S(1)}, u32[]{:S(2)}, u32[]{:S(2)}) collective-permute-start(bf16[1,128,768]{2,1,0:T(8,128)(2,1)S(1)} %get-tuple-element.51), channel_id=1, source_target_pairs={{0,1},{1,0},{2,3},{3,2},{4,5},{5,4},{6,7},{7,6},{8,9},{9,8},{10,11... | collective-permute-start | bytes 589832 | tf_op jit(solution)/shard_map/ppermute | solution.py:27
  60.0 14.3 %collective-permute-start.16 = (bf16[2,128,768]{2,1,0:T(8,128)(2,1)S(1)}, bf16[2,128,768]{2,1,0:T(8,128)(2,1)S(1)}, u32[]{:S(2)}, u32[]{:S(2)}) collective-permute-start(bf16[2,128,768]{2,1,0:T(8,128)(2,1)S(1)} %pad_maximum_fusion.16), channel_id=1, source_target_pairs={{0,1},{1,0},{2,3},{3,2},{4,5},{5,4},{6,7},{7,6},{8,9},{9,8},{10,11... | collective-permute-start | bytes 1179656 | tf_op jit(solution)/shard_map/ppermute | solution.py:27
  68.7 31.9 %collective-permute-start.1 = (bf16[2,128,768]{2,1,0:T(8,128)(2,1)}, bf16[2,128,768]{2,1,0:T(8,128)(2,1)}, u32[]{:S(2)}, u32[]{:S(2)}) collective-permute-start(bf16[2,128,768]{2,1,0:T(8,128)(2,1)} %get-tuple-element.16), channel_id=1, source_target_pairs={{0,4},{4,0},{1,5},{5,1},{2,6},{6,2},{3,7},{7,3},{8,12},{12,8},{9,1... | collective-permute-start | bytes 1179656 | tf_op jit(solution)/shard_map/ppermute | solution.py:300
  68.8 25.1 %collective-permute-start.20 = (bf16[2,128,768]{2,1,0:T(8,128)(2,1)}, bf16[2,128,768]{2,1,0:T(8,128)(2,1)}, u32[]{:S(2)}, u32[]{:S(2)}) collective-permute-start(bf16[2,128,768]{2,1,0:T(8,128)(2,1)} %pad_maximum_fusion.20), channel_id=1, source_target_pairs={{0,4},{4,0},{1,5},{5,1},{2,6},{6,2},{3,7},{7,3},{8,12},{12,8},{9,1... | collective-permute-start | bytes 1179656 | tf_op jit(solution)/shard_map/ppermute | solution.py:344
  70.4 11.0 %collective-permute-start.10 = (bf16[2,128,768]{2,1,0:T(8,128)(2,1)S(1)}, bf16[2,128,768]{2,1,0:T(8,128)(2,1)S(1)}, u32[]{:S(2)}, u32[]{:S(2)}) collective-permute-start(bf16[2,128,768]{2,1,0:T(8,128)(2,1)S(1)} %pad_maximum_fusion.13), channel_id=1, source_target_pairs={{0,2},{1,3},{2,0},{3,1},{4,6},{5,7},{6,4},{7,5},{8,10},{9,11},{10,... | collective-permute-start | bytes 1179656 | tf_op jit(solution)/shard_map/ppermute | solution.py:27
  84.0 9.9 %collective-permute-start.21 = (bf16[2,128,768]{2,1,0:T(8,128)(2,1)}, bf16[2,128,768]{2,1,0:T(8,128)(2,1)}, u32[]{:S(2)}, u32[]{:S(2)}) collective-permute-start(bf16[2,128,768]{2,1,0:T(8,128)(2,1)} %pad_maximum_fusion.21), channel_id=1, source_target_pairs={{0,4},{4,0},{1,5},{5,1},{2,6},{6,2},{3,7},{7,3},{8,12},{12,8},{9,1... | collective-permute-start | bytes 1179656 | tf_op jit(solution)/shard_map/ppermute | solution.py:344
  84.8 9.6 %collective-permute-start.22 = (bf16[2,128,768]{2,1,0:T(8,128)(2,1)}, bf16[2,128,768]{2,1,0:T(8,128)(2,1)}, u32[]{:S(2)}, u32[]{:S(2)}) collective-permute-start(bf16[2,128,768]{2,1,0:T(8,128)(2,1)} %pad_maximum_fusion.22), channel_id=1, source_target_pairs={{0,4},{4,0},{1,5},{5,1},{2,6},{6,2},{3,7},{7,3},{8,12},{12,8},{9,1... | collective-permute-start | bytes 1179656 | tf_op jit(solution)/shard_map/ppermute | solution.py:344
  88.5 4.1 %copy-start.17 = (bf16[1,128,768]{2,1,0:T(8,128)(2,1)S(1)}, bf16[1,128,768]{2,1,0:T(8,128)(2,1)}, u32[]{:S(2)}) copy-start(bf16[1,128,768]{2,1,0:T(8,128)(2,1)} %get-tuple-element.58) | copy-start | bytes 589828
  88.5 4.2 %copy-start.18 = (bf16[1,128,768]{2,1,0:T(8,128)(2,1)S(1)}, bf16[1,128,768]{2,1,0:T(8,128)(2,1)}, u32[]{:S(2)}) copy-start(bf16[1,128,768]{2,1,0:T(8,128)(2,1)} %get-tuple-element.54) | copy-start | bytes 589828
  88.5 5.3 %copy-start.19 = (bf16[1,128,768]{2,1,0:T(8,128)(2,1)S(1)}, bf16[1,128,768]{2,1,0:T(8,128)(2,1)}, u32[]{:S(2)}) copy-start(bf16[1,128,768]{2,1,0:T(8,128)(2,1)} %get-tuple-element.31) | copy-start | bytes 589828
  88.5 6.1 %copy-start.6 = (bf16[1,4,128,768]{3,2,1,0:T(8,128)(2,1)S(1)}, bf16[1,4,128,768]{3,2,1,0:T(8,128)(2,1)}, u32[]{:S(2)}) copy-start(bf16[1,4,128,768]{3,2,1,0:T(8,128)(2,1)} %get-tuple-element.45) | copy-start | bytes 2359300
  88.5 6.1 %copy-start.7 = (bf16[1,4,128,768]{3,2,1,0:T(8,128)(2,1)S(1)}, bf16[1,4,128,768]{3,2,1,0:T(8,128)(2,1)}, u32[]{:S(2)}) copy-start(bf16[1,4,128,768]{3,2,1,0:T(8,128)(2,1)} %get-tuple-element.43) | copy-start | bytes 2359300
  92.6 1.9 copy-start.3
  92.6 1.9 copy-start.4
  92.6 1.9 copy-start.5
  93.9 5.6 %collective-permute-start.17 = (bf16[2,128,768]{2,1,0:T(8,128)(2,1)S(1)}, bf16[2,128,768]{2,1,0:T(8,128)(2,1)S(1)}, u32[]{:S(2)}, u32[]{:S(2)}) collective-permute-start(bf16[2,128,768]{2,1,0:T(8,128)(2,1)S(1)} %pad_maximum_fusion.17), channel_id=1, source_target_pairs={{0,4},{4,0},{1,5},{5,1},{2,6},{6,2},{3,7},{7,3},{8,12},{12,8},{9,1... | collective-permute-start | bytes 1179656 | tf_op jit(solution)/shard_map/ppermute | solution.py:343
  94.0 5.5 %collective-permute-start.18 = (bf16[2,128,768]{2,1,0:T(8,128)(2,1)S(1)}, bf16[2,128,768]{2,1,0:T(8,128)(2,1)S(1)}, u32[]{:S(2)}, u32[]{:S(2)}) collective-permute-start(bf16[2,128,768]{2,1,0:T(8,128)(2,1)S(1)} %pad_maximum_fusion.18), channel_id=1, source_target_pairs={{0,4},{4,0},{1,5},{5,1},{2,6},{6,2},{3,7},{7,3},{8,12},{12,8},{9,1... | collective-permute-start | bytes 1179656 | tf_op jit(solution)/shard_map/ppermute | solution.py:343
  94.5 5.0 %collective-permute-start.19 = (bf16[2,128,768]{2,1,0:T(8,128)(2,1)S(1)}, bf16[2,128,768]{2,1,0:T(8,128)(2,1)S(1)}, u32[]{:S(2)}, u32[]{:S(2)}) collective-permute-start(bf16[2,128,768]{2,1,0:T(8,128)(2,1)S(1)} %pad_maximum_fusion.19), channel_id=1, source_target_pairs={{0,4},{4,0},{1,5},{5,1},{2,6},{6,2},{3,7},{7,3},{8,12},{12,8},{9,1... | collective-permute-start | bytes 1179656 | tf_op jit(solution)/shard_map/ppermute | solution.py:343
  171.6 5.8 %copy-start.1 = (bf16[3,768,768]{2,1,0:T(8,128)(2,1)S(1)}, bf16[3,768,768]{2,1,0:T(8,128)(2,1)}, u32[]{:S(2)}) copy-start(bf16[3,768,768]{2,1,0:T(8,128)(2,1)} %gradient.1) | copy-start | bytes 10616836
  174.1 2.4 %collective-permute-start.23 = (bf16[3,128,768]{2,1,0:T(8,128)(2,1)}, bf16[3,128,768]{2,1,0:T(8,128)(2,1)}, u32[]{:S(2)}, u32[]{:S(2)}) collective-permute-start(bf16[3,128,768]{2,1,0:T(8,128)(2,1)} %get-tuple-element.7), channel_id=1, source_target_pairs={{0,4},{4,0},{1,5},{5,1},{2,6},{6,2},{3,7},{7,3},{8,12},{12,8},{9,1... | collective-permute-start | bytes 1769480 | tf_op jit(solution)/shard_map/ppermute | solution.py:411
  174.5 2.8 %collective-permute-start.24 = (bf16[3,128,768]{2,1,0:T(8,128)(2,1)}, bf16[3,128,768]{2,1,0:T(8,128)(2,1)}, u32[]{:S(2)}, u32[]{:S(2)}) collective-permute-start(bf16[3,128,768]{2,1,0:T(8,128)(2,1)} %get-tuple-element.8), channel_id=1, source_target_pairs={{0,4},{4,0},{1,5},{5,1},{2,6},{6,2},{3,7},{7,3},{8,12},{12,8},{9,1... | collective-permute-start | bytes 1769480 | tf_op jit(solution)/shard_map/ppermute | solution.py:412
  174.6 4.3 %slice-start = ((bf16[3,768,768]{2,1,0:T(8,128)(2,1)}), bf16[3,256,768]{2,1,0:T(8,128)(2,1)S(1)}, s32[]{:S(2)}) async-start(bf16[3,768,768]{2,1,0:T(8,128)(2,1)} %gradient.1), calls=%async_computation | async-start | bytes 2359296 | tf_op jit(solution)/shard_map/slice | solution.py:416
  179.2 16.3 %collective-permute-start.25 = (bf16[3,128,768]{2,1,0:T(8,128)(2,1)S(1)}, bf16[3,128,768]{2,1,0:T(8,128)(2,1)S(1)}, u32[]{:S(2)}, u32[]{:S(2)}) collective-permute-start(bf16[3,128,768]{2,1,0:T(8,128)(2,1)S(1)} %get-tuple-element.9), channel_id=1, source_target_pairs={{0,1},{1,0},{2,3},{3,2},{4,5},{5,4},{6,7},{7,6},{8,9},{9,8},{10,11... | collective-permute-start | bytes 1769480 | tf_op jit(solution)/shard_map/ppermute | solution.py:427
  180.7 28.0 %collective-permute-start.26 = (bf16[3,128,768]{2,1,0:T(8,128)(2,1)S(1)}, bf16[3,128,768]{2,1,0:T(8,128)(2,1)S(1)}, u32[]{:S(2)}, u32[]{:S(2)}) collective-permute-start(bf16[3,128,768]{2,1,0:T(8,128)(2,1)S(1)} %get-tuple-element.11), channel_id=1, source_target_pairs={{0,2},{1,3},{2,0},{3,1},{4,6},{5,7},{6,4},{7,5},{8,10},{9,11},{10,... | collective-permute-start | bytes 1769480 | tf_op jit(solution)/shard_map/ppermute | solution.py:427
  181.2 27.4 %collective-permute-start.27 = (bf16[3,128,768]{2,1,0:T(8,128)(2,1)S(1)}, bf16[3,128,768]{2,1,0:T(8,128)(2,1)S(1)}, u32[]{:S(2)}, u32[]{:S(2)}) collective-permute-start(bf16[3,128,768]{2,1,0:T(8,128)(2,1)S(1)} %get-tuple-element.10), channel_id=1, source_target_pairs={{0,3},{1,2},{2,1},{3,0},{4,7},{5,6},{6,5},{7,4},{8,11},{9,10},{10,... | collective-permute-start | bytes 1769480 | tf_op jit(solution)/shard_map/ppermute | solution.py:427
  (4 other events, 4.0 us)

commit v2 on v1

v2 whole, which is shorter than its diff:
```python
import functools

import jax
import jax.numpy as jnp
from jax import lax
from jax.experimental import pallas as pl
from jax.experimental.pallas import tpu as pltpu
from jax.sharding import PartitionSpec as P

MARGIN = 128
LANES = 128
CHUNK = 64
ALIGN = 16
F32 = jnp.float32
BF16 = jnp.bfloat16
VMEM_LIMIT = 62 * 1024 * 1024


def ring(count, by):
    return [(i, (i + by) % count) for i in range(count)]


def swapped(x, axis, bit):
    return lax.ppermute(x, axis, [(i, i ^ bit) for i in range(lax.axis_size(axis))])


def low_bit(j):
    return j & -j


def high_bit(j):
    return 1 << (j.bit_length() - 1)


def spread(piece):
    count = lax.axis_size("probe")
    whole = {0: piece}
    for i in range(1, count):
        if low_bit(i) == i:
            whole[i] = swapped(piece, "probe", i)
    real = {i: value[0] for i, value in whole.items()}
    imag = {i: value[1] for i, value in whole.items()}
    held = []
    for i in range(count):
        if i in whole:
            held.append((whole[i],))
        else:
            real[i] = swapped(real[i ^ high_bit(i)], "probe", high_bit(i))
            imag[i] = swapped(imag[i ^ low_bit(i)], "probe", low_bit(i))
            held.append((real[i], imag[i]))
    return held


def dot(a, b):
    return jnp.dot(a, b, preferred_element_type=F32)


def into_rows(parts, target, first, rows, sem):
    span = pl.ds(first, rows)
    if len(parts) == 1:
        return [pltpu.make_async_copy(parts[0], target.at[:, span, :], sem)]
    return [
        pltpu.make_async_copy(part, target.at[comp, span, :], sem)
        for comp, part in enumerate(parts)
    ]


def nested(structure, flat):
    refs = iter(flat)
    return [tuple(next(refs) for _ in range(n)) for n in structure]


def pick_body(structure, info, *refs):
    held = nested(structure, refs)
    out, sem = refs[-2:]
    place = info[1]
    piece_rows = held[0][0].shape[-2]
    count = len(held)
    needed = MARGIN // piece_rows
    for act in (True, False):
        for i, parts in enumerate(held):
            index = place ^ i
            for edge, begin in ((0, count - needed), (1, 0)):

                @pl.when((index >= begin) & (index < begin + needed))
                def _():
                    first = pl.multiple_of((index - begin) * piece_rows, ALIGN)
                    for copy in into_rows(parts, out.at[edge], first, piece_rows, sem.at[0]):
                        copy.start() if act else copy.wait()


def edges(info, held):
    flat = [part for parts in held for part in parts]
    width = flat[0].shape[-1]
    return pl.pallas_call(
        functools.partial(pick_body, tuple(len(parts) for parts in held)),
        out_shape=jax.ShapeDtypeStruct((2, 2, MARGIN, width), BF16),
        in_specs=[pl.BlockSpec(memory_space=pltpu.SMEM)]
        + [pl.BlockSpec(memory_space=pl.ANY)] * len(flat),
        out_specs=pl.BlockSpec(memory_space=pltpu.VMEM),
        scratch_shapes=[pltpu.SemaphoreType.DMA((1,))],
        compiler_params=pltpu.CompilerParams(vmem_limit_bytes=8 * 1024 * 1024),
        cost_estimate=pl.CostEstimate(flops=0, bytes_accessed=1 << 21, transcendentals=0),
        name="edges",
    )(info, *flat)


def across_tiles(both):
    tiles = lax.axis_size("tile")
    if tiles == 2:
        moved = lax.ppermute(both, "tile", ring(tiles, 1))
        return (moved,)
    return (
        lax.ppermute(both[0], "tile", ring(tiles, 1)),
        lax.ppermute(both[1], "tile", ring(tiles, -1)),
    )


def run_body(final, structure, slice_count, info, starts, *refs):
    held_structure, margin_count = structure
    refs = list(refs)

    def take(n):
        taken = refs[:n]
        del refs[:n]
        return taken

    own = take(1)[0]
    margins = [take(margin_count) for _ in range(len(held_structure) + 1)]
    slots = [nested(shape, take(sum(shape))) for shape in held_structure]
    mat_sources = take(4 if final else 2)
    if final:
        begun_wave, begun_wins, begun_saved, measured = take(4)
        out = take(1)[0]
        wave, saved = take(2)
    else:
        probe = take(1)[0]
        wave, wins_out, saved = take(3)
    stage, wins, work, middle, mats = take(5)
    if final:
        amplitude, grid = take(2)
    else:
        probe_v = take(1)[0]
    sem_stage, sem_mat, sem_in = take(3)

    mine, place = info[0], info[1]
    k_first, k_last = (info[2], slice_count) if final else (0, info[2])
    count, size = wave.shape[0], wave.shape[2]
    own_rows, width = own.shape[1], own.shape[2]
    tall = own_rows + 2 * MARGIN
    pieces = len(held_structure[0])
    piece_rows = own_rows // pieces
    lanes = size + LANES
    col_last = (width - size) // LANES - 1
    steps = size // CHUNK

    def stage_start(k):
        slot = lax.rem(k, 2)
        target = stage.at[slot]
        sem = sem_stage.at[slot]

        def margins_in(j):
            if margin_count == 1:
                above, below = margins[j][0].at[0], margins[j][0].at[1]
            else:
                above, below = margins[j]
            return into_rows((above,), target, 0, MARGIN, sem) + into_rows(
                (below,), target, MARGIN + own_rows, MARGIN, sem
            )

        @pl.when((k ^ mine) == 0)
        def _():
            for copy in margins_in(0) + into_rows((own,), target, MARGIN, own_rows, sem):
                copy.start()

        for j in range(1, len(slots) + 1):

            @pl.when((k ^ mine) == j)
            def _():
                for copy in margins_in(j):
                    copy.start()
                for i, parts in enumerate(slots[j - 1]):
                    first = pl.multiple_of(MARGIN + (place ^ i) * piece_rows, ALIGN)
                    for copy in into_rows(parts, target, first, piece_rows, sem):
                        copy.start()

    def stage_wait(k):
        slot = lax.rem(k, 2)
        whole = stage.at[slot, :, pl.ds(0, tall), :]
        pltpu.make_async_copy(whole, whole, sem_stage.at[slot]).wait()

    def span(i, rows=CHUNK, offset=0):
        return pl.ds(pl.multiple_of(i * rows + offset, 8), rows)

    mat_copies = [
        pltpu.make_async_copy(source, mats.at[i], sem_mat.at[i])
        for i, source in enumerate(mat_sources)
    ]

    @pl.when(k_first < k_last)
    def _():
        stage_start(jnp.int32(k_first))

    if final:
        wave_copy = pltpu.make_async_copy(begun_wave, wave, sem_in.at[0])
        saved_copy = pltpu.make_async_copy(begun_saved, saved, sem_in.at[1])
        measured_copy = pltpu.make_async_copy(measured, amplitude, sem_in.at[2])
        wave_copy.start()
    else:
        probe_copy = pltpu.make_async_copy(probe, probe_v, sem_in.at[0])
        probe_copy.start()
    for copy in mat_copies[:2]:
        copy.start()
    if final:
        saved_copy.start()
        measured_copy.start()
        for copy in mat_copies[2:]:
            copy.start()

        def wins_start(k, _):
            pltpu.make_async_copy(begun_wins.at[k], wins.at[k], sem_in.at[3]).start()
            return 0

        def wins_wait(k, _):
            pltpu.make_async_copy(begun_wins.at[k], wins.at[k], sem_in.at[3]).wait()
            return 0

        lax.fori_loop(0, k_first, wins_start, 0)

        def clear(i, _):
            for comp in range(3):
                grid[comp, span(i, 8), :] = jnp.zeros((8, width), F32)
            return 0

        lax.fori_loop(0, grid.shape[1] // 8, clear, 0)
        wave_copy.wait()
        saved_copy.wait()
    else:
        probe_copy.wait()

        def fill(i, _):
            for comp in range(2):
                value = probe_v[comp, span(i), :]
                for position in range(count):
                    wave[position, span(i, CHUNK, comp * size), :] = value
            return 0

        lax.fori_loop(0, steps, fill, 0)

    def column(position):
        col = starts[position, 1]
        tile = jnp.minimum(col // LANES, col_last)
        return pl.multiple_of(tile * LANES, LANES), col - tile * LANES

    def rolled_rows(x, shift, keep):
        groups = x.shape[0] // 8
        turned = pltpu.roll(x.reshape(groups, 8, x.shape[1]), lax.rem(8 - shift, 8), 1)
        row = lax.broadcasted_iota(jnp.int32, (1, 8, x.shape[1]), 1)
        kept = keep // 8
        return jnp.where(row < 8 - shift, turned[:kept], turned[1 : kept + 1]).reshape(
            keep, x.shape[1]
        )

    def rolled_lanes(x, shift):
        back = lax.rem(LANES - shift, LANES)
        tiles = [x[:, j * LANES : (j + 1) * LANES] for j in range(x.shape[1] // LANES)]
        turned = [pltpu.roll(tile, back, 1) for tile in tiles]
        lane = lax.broadcasted_iota(jnp.int32, (1, LANES), 1)
        mask = lane < LANES - shift
        return jnp.concatenate(
            [jnp.where(mask, a, b) for a, b in zip(turned[:-1], turned[1:])], axis=1
        )

    def spread_lanes(x, shift):
        turn = lax.rem(shift, LANES)
        tiles = [x[:, j * LANES : (j + 1) * LANES] for j in range(x.shape[1] // LANES)]
        turned = [pltpu.roll(tile, turn, 1) for tile in tiles]
        lane = lax.broadcasted_iota(jnp.int32, (1, LANES), 1)
        mask = lane < shift
        nothing = jnp.zeros_like(turned[0])
        return jnp.concatenate(
            [jnp.where(mask, a, b) for a, b in zip([nothing] + turned, turned + [nothing])], axis=1
        )

    def spread_rows(x, shift):
        groups = x.shape[0] // 8
        turned = pltpu.roll(x.reshape(groups, 8, x.shape[1]), shift, 1)
        nothing = jnp.zeros((1, 8, x.shape[1]), F32)
        row = lax.broadcasted_iota(jnp.int32, (1, 8, x.shape[1]), 1)
        return jnp.where(
            row < shift,
            jnp.concatenate([nothing, turned], axis=0),
            jnp.concatenate([turned, nothing], axis=0),
        ).reshape(x.shape[0] + 8, x.shape[1])

    def add_piece(position, comp, i, value):
        row = starts[position, 0] + i * CHUNK
        inside = lax.rem(row, 8)
        first = pl.multiple_of(row - inside, 8)
        col_first, shift = column(position)
        wide = spread_lanes(value, shift)
        grid[comp, pl.ds(first, CHUNK + 8), pl.ds(col_first, lanes)] += spread_rows(wide, inside)

    def halves(position, i):
        return (
            wave[position, span(i), :].astype(F32),
            wave[position, span(i, CHUNK, size), :].astype(F32),
        )

    def put_work(position, i, real, imag):
        work[position, span(i), pl.ds(0, size)] = real.astype(BF16)
        work[position, span(i), pl.ds(size, size)] = imag.astype(BF16)

    def propagate(position, col, row):
        for n in range(2):
            part = dot(work[position], mats[col, :, pl.ds(n * size, size)])
            middle[position, pl.ds(n * size, size), :] = part.astype(BF16)
        for m in range(2):
            part = dot(mats[row, pl.ds(m * size, size), :], middle[position])
            wave[position, pl.ds(m * size, size), :] = part.astype(BF16)

    def forward(k, _):
        slot = lax.rem(k, 2)
        stage_wait(k)

        @pl.when(k + 1 < k_last)
        def _():
            stage_start(k + 1)

        @pl.when(k == mine)
        def _():
            for position in range(count):
                for comp in range(2):
                    rows = pl.ds(comp * size, size)
                    saved[position, rows, :] = wave[position, rows, :]

        for position in range(count):
            row_start = starts[position, 0]
            col_first, shift = column(position)
            inside = lax.rem(row_start, ALIGN)
            fine = lax.rem(inside, 8)
            lower = inside >= 8

            def enter(i, _):
                first = pl.multiple_of(row_start - inside + i * CHUNK, ALIGN)

                def window(comp):
                    block = stage[
                        slot, comp, pl.ds(first, CHUNK + ALIGN), pl.ds(col_first, lanes)
                    ].astype(F32)
                    block = jnp.where(lower, block[8:], block[:-8])
                    return rolled_lanes(rolled_rows(block, fine, CHUNK), shift)

                win_real, win_imag = window(0), window(1)
                wins[k, position, 0, span(i), :] = win_real.astype(BF16)
                wins[k, position, 1, span(i), :] = win_imag.astype(BF16)
                real, imag = halves(position, i)
                put_work(
                    position,
                    i,
                    real * win_real - imag * win_imag,
                    real * win_imag + imag * win_real,
                )
                return 0

            lax.fori_loop(0, steps, enter, 0)

        if not final:
            pltpu.make_async_copy(wins.at[k], wins_out.at[k], sem_in.at[1]).start()

        @pl.when(k == k_first)
        def _():
            mat_copies[0].wait()
            mat_copies[1].wait()

        for position in range(count):
            propagate(position, 0, 1)
        return 0

    lax.fori_loop(k_first, k_last, forward, 0)

    if not final:

        @pl.when(k_last == 0)
        def _():
            mat_copies[0].wait()
            mat_copies[1].wait()

        def wins_sent(k, _):
            pltpu.make_async_copy(wins.at[k], wins_out.at[k], sem_in.at[1]).wait()
            return 0

        lax.fori_loop(0, k_last, wins_sent, 0)
        return

    measured_copy.wait()

    for position in range(count):

        def detect(i, _):
            real, imag = halves(position, i)
            seen = amplitude[position, span(i), :]
            factor = 1.0 - seen / jnp.sqrt(real * real + imag * imag + 1.0)
            put_work(position, i, real * factor, imag * factor)
            return 0

        lax.fori_loop(0, steps, detect, 0)

    mat_copies[2].wait()
    mat_copies[3].wait()
    lax.fori_loop(0, k_first, wins_wait, 0)

    def backward(step, _):
        k = slice_count - 1 - step
        for position in range(count):
            propagate(position, 2, 3)
        for position in range(count):

            @pl.when(k == mine)
            def _():
                def collect(i, _):
                    real, imag = halves(position, i)
                    old_real = saved[position, span(i), :].astype(F32)
                    old_imag = saved[position, span(i, CHUNK, size), :].astype(F32)
                    add_piece(position, 0, i, old_real * real + old_imag * imag)
                    add_piece(position, 1, i, old_real * imag - old_imag * real)
                    add_piece(position, 2, i, old_real * old_real + old_imag * old_imag)
                    return 0

                lax.fori_loop(0, steps, collect, 0)

            @pl.when(k != mine)
            def _():
                def leave(i, _):
                    real, imag = halves(position, i)
                    win_real = wins[k, position, 0, span(i), :].astype(F32)
                    win_imag = wins[k, position, 1, span(i), :].astype(F32)
                    put_work(
                        position,
                        i,
                        win_real * real + win_imag * imag,
                        win_real * imag - win_imag * real,
                    )
                    return 0

                lax.fori_loop(0, steps, leave, 0)

        return 0

    lax.fori_loop(0, slice_count - mine, backward, 0)

    def emit(i, _):
        for comp in range(3):
            out[comp, span(i, ALIGN), :] = grid[comp, span(i, ALIGN), :].astype(BF16)
        return 0

    lax.fori_loop(0, tall // ALIGN, emit, 0)


def block_matrix(real, imag):
    return jnp.concatenate(
        [jnp.concatenate([real, -imag], axis=1), jnp.concatenate([imag, real], axis=1)], axis=0
    )


def prefix_ready(section, slots, slice_count):
    ready, total = jnp.int32(1), jnp.int32(0)
    for k in range(slice_count):
        ready = ready * ((section ^ k) <= slots).astype(jnp.int32)
        total = total + ready
    return total


def scattered(folded, place, order):
    bits = len(order)
    rows = folded.shape[1] >> bits
    held = folded.reshape((folded.shape[0],) + (2,) * bits + (rows, folded.shape[2]))
    axes = {bit: 1 + bits - 1 - bit for bit in order}
    for bit in order:
        axis = axes.pop(bit)
        axes = {b: a - (a > axis) for b, a in axes.items()}
        side = (place >> bit) & 1
        mine = lax.dynamic_index_in_dim(held, side, axis, keepdims=False)
        other = lax.dynamic_index_in_dim(held, 1 - side, axis, keepdims=False)
        arrived = swapped(other.astype(BF16), "probe", 1 << bit)
        held = mine.astype(F32) + arrived.astype(F32)
    return held


def shards(probe_wave, fresnel_rows, fresnel_cols, object_slices, offsets, measured):
    cut_count = lax.axis_size("cuts")
    probe_count = lax.axis_size("probe")
    section = lax.axis_index("cuts")
    place = lax.axis_index("probe")
    owned = object_slices[0]
    own_count = owned.shape[1]
    width_cols = owned.shape[2]
    size = probe_wave.shape[1]
    count = offsets.shape[1]
    piece_rows = own_count // probe_count
    tall = own_count + 2 * MARGIN

    first_piece = lax.dynamic_slice_in_dim(owned, place * piece_rows, piece_rows, axis=1)
    first_piece = first_piece.astype(BF16)
    early_slots = max(cut_count - 2, 1)
    info = jnp.stack([section, place, prefix_ready(section, early_slots, cut_count)])
    info = info.astype(jnp.int32)
    slots = {0: first_piece}
    for j in range(1, cut_count):
        slots[j] = swapped(slots[j ^ low_bit(j)], "cuts", low_bit(j))
    own = owned.astype(BF16)
    own_edges = jnp.stack([own[:, own_count - MARGIN :], own[:, :MARGIN]])
    margins = [across_tiles(own_edges)]
    helds = []
    for j in range(1, cut_count):
        held = spread(slots[j])
        margins.append(across_tiles(edges(info, held)))
        helds.append(held)

    row_mat = block_matrix(fresnel_rows[0], fresnel_rows[1])
    col_mat_t = block_matrix(fresnel_cols[0], fresnel_cols[1])
    row_mat_t, col_mat = row_mat.T, col_mat_t.T

    anywhere = pl.BlockSpec(memory_space=pl.ANY)
    scalars = pl.BlockSpec(memory_space=pltpu.SMEM)
    vmem = pl.BlockSpec(memory_space=pltpu.VMEM)
    wave_shape = jax.ShapeDtypeStruct((count, 2 * size, size), BF16)
    prop_flops = 2 * count * 2 * (2 * size) ** 2 * size
    scratch = [
        pltpu.VMEM((2, 2, tall + ALIGN, width_cols), BF16),
        pltpu.VMEM((cut_count, count, 2, size, size), BF16),
        pltpu.VMEM((count, size, 2 * size), BF16),
        pltpu.VMEM((count, 2 * size, size), BF16),
    ]

    def run(final, used, extra, out_shape, out_specs, more, props):
        structure = tuple(tuple(len(parts) for parts in held) for held in helds[:used])
        inputs = [own] + [m for group in margins[: used + 1] for m in group]
        inputs += [part for held in helds[:used] for parts in held for part in parts]
        inputs += extra
        return pl.pallas_call(
            functools.partial(run_body, final, (structure, len(margins[0])), cut_count),
            out_shape=out_shape,
            in_specs=[scalars, scalars] + [anywhere] * len(inputs),
            out_specs=out_specs,
            scratch_shapes=more
            + [pltpu.SemaphoreType.DMA((2,)), pltpu.SemaphoreType.DMA((4,)), pltpu.SemaphoreType.DMA((4,))],
            compiler_params=pltpu.CompilerParams(vmem_limit_bytes=VMEM_LIMIT),
            cost_estimate=pl.CostEstimate(
                flops=props * prop_flops, bytes_accessed=1 << 24, transcendentals=0
            ),
            name="finish" if final else "begin",
        )(info, offsets[0], *inputs)

    wave, wins, saved = run(
        False,
        early_slots,
        [col_mat, row_mat, probe_wave],
        (
            wave_shape,
            jax.ShapeDtypeStruct((cut_count, count, 2, size, size), BF16),
            wave_shape,
        ),
        (vmem, anywhere, vmem),
        scratch
        + [pltpu.VMEM((2, 2 * size, 2 * size), BF16), pltpu.VMEM((2, size, size), BF16)],
        early_slots + 1,
    )
    grid = run(
        True,
        cut_count - 1,
        [col_mat, row_mat, col_mat_t, row_mat_t, wave, wins, saved, measured[0]],
        jax.ShapeDtypeStruct((3, tall, width_cols), BF16),
        vmem,
        [pltpu.VMEM(wave_shape.shape, BF16), pltpu.VMEM(wave_shape.shape, BF16)]
        + scratch
        + [
            pltpu.VMEM((4, 2 * size, 2 * size), BF16),
            pltpu.VMEM((count, size, size), F32),
            pltpu.VMEM((3, tall + 8, width_cols), F32),
        ],
        cut_count + 1,
    )

    tiles = lax.axis_size("tile")
    inside = grid[:, MARGIN : MARGIN + own_count]
    upper = lax.ppermute(grid[:, MARGIN + own_count :], "tile", ring(tiles, 1))
    lower = lax.ppermute(grid[:, :MARGIN], "tile", ring(tiles, -1))
    folded = jnp.concatenate(
        [
            inside[:, :MARGIN].astype(F32) + upper.astype(F32),
            inside[:, MARGIN : own_count - MARGIN].astype(F32),
            inside[:, own_count - MARGIN :].astype(F32) + lower.astype(F32),
        ],
        axis=1,
    ).astype(BF16)

    bits = list(range(probe_count.bit_length() - 1))
    half = width_cols // 2
    left = scattered(folded[:, :, :half], place, bits[::-1])
    right = scattered(folded[:, :, half:], place, bits)
    summed = jnp.concatenate([left, right], axis=-1)
    own_part = lax.dynamic_slice_in_dim(owned, place * piece_rows, piece_rows, 1)
    updated = own_part - summed[:2] / (summed[2] + 1.0)
    return updated[None]


def solution(mesh):
    in_specs = (
        P(),
        P(),
        P(),
        P("cuts", None, "tile", None),
        P("tile", "probe", None),
        P("tile", "probe", None, None),
    )
    out_specs = P("cuts", None, ("tile", "probe"), None)
    return jax.shard_map(shards, mesh=mesh, in_specs=in_specs, out_specs=out_specs, check_vma=False)
```

time: 212 us -> 186 us (0.88)
  waiting for transfers between devices: 64.4 us -> 42.1 us
  other arithmetic: 29.9 us -> 16.7 us
  local copies, waits for them, and re-layouts: 19.4 us -> 28.7 us
  between operations: 3.92 us -> 0.43 us
  starting transfers between devices: 22.7 us -> 25.6 us
    ppermute x26 -> x23, waiting for transfers between devices: 61.7 us -> 39.3 us  [the longest x19 39.3 us: swapped(): lax.ppermute(x, axis, [(i, i ^ bit) for i in range(lax.axis_size(axis))])]
    another operation x11 -> x3, other arithmetic: 11.8 us -> 3.78 us  [the longest x1 2.19 us: shards(): own_edges = jnp.stack([own[:, own_count - MARGIN:], own[:, :MARGIN]])]
    concatenate x13 -> x1, other arithmetic: 9.94 us -> 3.98 us  [block_matrix(): jnp.concatenate([jnp.concatenate([real, -imag], axis=1), jnp.concatenate(...]
    squeeze x1 -> x7, local copies, waits for them, and re-layouts: 0.07 us -> 4.77 us  [the longest x3 2.22 us: spread(): imag = {i: value[1] for i, value in whole.items()}]
    dynamic_slice x6 -> x4, local copies, waits for them, and re-layouts: 4.01 us -> 0.4 us  [the longest x2 0.27 us: scattered(): mine = lax.dynamic_index_in_dim(held, side, axis, keepdims=False)]
    unnamed x48 -> x52, local copies, waits for them, and re-layouts: 3.94 us -> 7.3 us
    ppermute x26 -> x23, starting transfers between devices: 22.2 us -> 25.1 us  [the longest x19 24.3 us: swapped(): lax.ppermute(x, axis, [(i, i ^ bit) for i in range(lax.axis_size(axis))])]
    pallas_call x1 -> x5, Pallas kernels: 70.9 us -> 71.7 us  [the longest x2 67 us: run(): pl.pallas_call(functools.partial(run_body, final, (structure, len(margins...]
  transfers between devices with their start and end apart: 28 -> 25, of which waited for: 15 -> 10; matrix products, arithmetic and copies ran while one was open for 17% -> 17% of each run, Pallas kernels for 0% -> 17%
where the time goes in v2:
time: 186 us; the launch traced here: 185 us
  Pallas kernels  71.7 us (39%)
  waiting for transfers between devices  42.1 us (23%)
  local copies, waits for them, and re-layouts  28.7 us (15%)
  starting transfers between devices  25.6 us (14%)
  other arithmetic  16.7 us (9%)
    pallas_call x2, Pallas kernels, run(): pl.pallas_call(functools.partial(run_body, final, (structure, len(margins...  67 us
    ppermute x19, waiting for transfers between devices, swapped(): lax.ppermute(x, axis, [(i, i ^ bit) for i in range(lax.axis_size(axis))])  39.3 us
    ppermute x19, starting transfers between devices, swapped(): lax.ppermute(x, axis, [(i, i ^ bit) for i in range(lax.axis_size(axis))])  24.3 us
    unnamed x52, local copies, waits for them, and re-layouts  7.3 us
    pallas_call x3, Pallas kernels, edges(): pl.pallas_call(functools.partial(pick_body, tuple((len(parts) for parts i...  4.65 us
    concatenate x1, local copies, waits for them, and re-layouts, block_matrix(): jnp.concatenate([jnp.concatenate([real, -imag], axis=1), jnp.concatenate(...  3.99 us
    concatenate x1, other arithmetic, block_matrix(): jnp.concatenate([jnp.concatenate([real, -imag], axis=1), jnp.concatenate(...  3.98 us
    transpose x1, local copies, waits for them, and re-layouts, shards(): row_mat_t, col_mat = (row_mat.T, col_mat_t.T)  3.94 us
  transfers between devices with their start and end apart: 25, of which 10 were waited for; matrix products, arithmetic and copies ran while one was open for 17% of the time, Pallas kernels for 17%

profile of v2, /device:TPU:0, one launch (start us, length us, event | category | flops | bytes accessed | tf_op | source)
XLA Modules:
  0.0 185.3 jit_solution(11179134211232290946)
XLA Ops:
  0.0 1.9 %bitcast_convert_fusion = bf16[2,128,768]{2,1,0:T(8,128)(2,1)} fusion(f32[1,2,512,768]{3,2,1,0:T(8,128)} %param.9, s32[]{:T(128)S(6)} %select_n.23), kind=kLoop, calls=%fused_computation.15 | loop fusion | bytes 786436 | tf_op jit(solution)/shard_map/convert_element_type | solution.py:504
  1.9 4.1 %collective-permute-start.7 = (bf16[2,128,768]{2,1,0:T(8,128)(2,1)}, bf16[2,128,768]{2,1,0:T(8,128)(2,1)S(1)}, u32[]{:S(2)}, u32[]{:S(2)}) collective-permute-start(bf16[2,128,768]{2,1,0:T(8,128)(2,1)} %bitcast_convert_fusion), channel_id=1, source_target_pairs={{0,16},{8,24},{16,0},{24,8},{1,17},{9,25},{17,1},{25,9},{2,18},{10... | collective-permute-start | bytes 1179656 | tf_op jit(solution)/shard_map/ppermute | solution.py:24
  6.0 1.6 collective-permute-start.1
  7.6 2.0 %convert_bitcast_fusion.refs_0_ = bf16[2,512,768]{2,1,0:T(8,128)(2,1)S(1)} fusion(f32[1,2,512,768]{3,2,1,0:T(8,128)} %param.9), kind=kLoop, calls=%fused_computation.3 | loop fusion | flops 786432 | bytes 4718592 | tf_op jit(solution)/shard_map/convert_element_type | solution.py:511
  9.6 2.6 %fusion.13 = (bf16[1,512,512]{2,1,0:T(8,128)(2,1)S(1)}, bf16[1,512,512]{2,1,0:T(8,128)(2,1)}) fusion(bf16[2,512,512]{2,1,0:T(8,128)(2,1)} %param.7), kind=kLoop, calls=%fused_computation.50 | loop fusion | bytes 2097152 | tf_op jit(solution)/shard_map/slice | solution.py:520
  12.5 1.0 slice_bitcast_fusion.3
  13.5 0.7 copy-done.21
  14.2 1.1 slice_bitcast_fusion
  15.2 8.6 %collective-permute-done.7.refs_0_.refs_9_.refs_10_ = bf16[2,128,768]{2,1,0:T(8,128)(2,1)S(1)} collective-permute-done((bf16[2,128,768]{2,1,0:T(8,128)(2,1)}, bf16[2,128,768]{2,1,0:T(8,128)(2,1)S(1)}, u32[]{:S(2)}, u32[]{:S(2)}) %collective-permute-start.7) | collective-permute-done | bytes 393248 | tf_op jit(solution)/shard_map/ppermute | solution.py:24
  23.8 1.5 collective-permute-start.8
  25.4 0.8 fusion.8
  26.2 1.5 collective-permute-start.9
  27.7 0.8 bitcast_negate_fusion
  30.3 5.5 %collective-permute-done.8.refs_1_.refs_10_.refs_11_ = bf16[2,128,768]{2,1,0:T(8,128)(2,1)S(1)} collective-permute-done((bf16[2,128,768]{2,1,0:T(8,128)(2,1)S(1)}, bf16[2,128,768]{2,1,0:T(8,128)(2,1)S(1)}, u32[]{:S(2)}, u32[]{:S(2)}) %collective-permute-start.8) | collective-permute-done | bytes 393248 | tf_op jit(solution)/shard_map/ppermute | solution.py:24
  35.8 1.6 collective-permute-start.10
  38.2 0.7 slice_bitcast_fusion.6
  38.9 0.8 collective-permute-start.11
  39.7 4.5 %collective-permute-done.2.refs_1_.refs_5_.refs_6_ = bf16[2,128,768]{2,1,0:T(8,128)(2,1)S(1)} collective-permute-done((bf16[2,128,768]{2,1,0:T(8,128)(2,1)S(1)}, bf16[2,128,768]{2,1,0:T(8,128)(2,1)S(1)}, u32[]{:S(2)}, u32[]{:S(2)}) %collective-permute-start.2) | collective-permute-done | bytes 393248 | tf_op jit(solution)/shard_map/ppermute | solution.py:24
  44.3 0.7 slice_bitcast_fusion.9
  45.0 1.6 collective-permute-start.4
  47.4 1.4 collective-permute-start.5
  49.5 2.1 %copy.23 = bf16[1,512,512]{1,2,0:T(8,128)(2,1)} copy(bf16[1,512,512]{2,1,0:T(8,128)(2,1)} %get-tuple-element.28) | data formatting | bytes 1048576
  51.5 2.2 %pad_maximum_fusion.1 = bf16[2,2,128,768]{3,2,1,0:T(8,128)(2,1)} fusion(bf16[1,2,128,768]{3,2,1,0:T(8,128)(2,1)} %get-tuple-element.22, bf16[1,2,128,768]{3,2,1,0:T(8,128)(2,1)} %get-tuple-element.21), kind=kLoop, calls=%fused_computation.14 | loop fusion | flops 393216 | bytes 1572864 | tf_op jit(solution)/shard_map/stack | solution.py:512
  54.5 1.5 collective-permute-start.15
  56.0 1.0 copy-done.7
  57.0 0.9 copy-done.12
  58.0 1.3 edges.4
  59.6 1.8 edges.3
  61.8 2.6 %fusion.9 = (bf16[1024,1024]{1,0:T(8,128)(2,1)}, bf16[1024,1024]{0,1:T(8,128)(2,1)}) fusion(bf16[512,512]{0,1:T(8,128)(2,1)S(1)} %bitcast.72, bf16[512,512]{0,1:T(8,128)(2,1)S(1)} %bitcast.71, bf16[512,512]{0,1:T(8,128)(2,1)S(1)} %copy-done.23), kind=kLoop, calls=%fused_computation.46 | loop fusion | flops 8388608 | bytes 5767168 | tf_op jit(solution)/shard_map/transpose | solution.py:522
  64.3 4.0 %copy.18.refs_15_.refs_21_ = bf16[1024,1024]{1,0:T(8,128)(2,1)} copy(bf16[1024,1024]{0,1:T(8,128)(2,1)} %get-tuple-element.18) | data formatting | bytes 4194304 | tf_op jit(solution)/shard_map/concatenate | solution.py:461
  68.3 0.7 slice_bitcast_fusion.5
  69.1 0.8 slice_bitcast_fusion.4
  69.8 1.9 %collective-permute-start.17 = (bf16[128,768]{1,0:T(8,128)(2,1)}, bf16[128,768]{1,0:T(8,128)(2,1)S(1)}, u32[]{:S(2)}, u32[]{:S(2)}) collective-permute-start(bf16[128,768]{1,0:T(8,128)(2,1)} %slice_bitcast_fusion.4), channel_id=1, source_target_pairs={{0,1},{1,0},{2,3},{3,2},{4,5},{5,4},{6,7},{7,6},{8,9},{9,8},{10,11... | collective-permute-start | bytes 589832 | tf_op jit(solution)/shard_map/ppermute | solution.py:24
  71.8 4.0 %maximum_maximum_fusion = (bf16[1024,1024]{1,0:T(8,128)(2,1)}, bf16[1024,1024]{0,1:T(8,128)(2,1)}) fusion(bf16[512,512]{1,0:T(8,128)(2,1)} %get-tuple-element.30, bf16[512,512]{1,0:T(8,128)(2,1)} %get-tuple-element.29, bf16[512,512]{1,0:T(8,128)(2,1)S(1)} %copy-done.22), kind=kLoop, calls=%fused_computation.1 | loop fusion | flops 8388608 | bytes 5767168 | tf_op jit(solution)/shard_map/concatenate | solution.py:461
  75.7 3.9 %copy.17.refs_14_.refs_20_ = bf16[1024,1024]{1,0:T(8,128)(2,1)} copy(bf16[1024,1024]{0,1:T(8,128)(2,1)} %get-tuple-element.20) | data formatting | bytes 4194304 | tf_op jit(solution)/shard_map/transpose | solution.py:522
  80.4 0.9 copy-done.15
  81.4 1.6 edges.5
  83.0 27.1 %begin.1 = (bf16[2,1024,512]{2,1,0:T(8,128)(2,1)}, bf16[4,2,2,512,512]{4,3,2,1,0:T(8,128)(2,1)}, bf16[2,1024,512]{2,1,0:T(8,128)(2,1)}) custom-call(s32[3]{0:T(128)} %copy-done.16, s32[2,2]{1,0:T(2,128)} %bitcast.76, bf16[2,512,768]{2,1,0:T(8,128)(2,1)} %copy-done.20, bf16[2,2,128,768]{3,2,1,0:T(8,128)(2,1)} %collective-permute-done.refs_1_, ...), custom_call_target="tpu_custom_call" | custom-call | flops 12884901888 | bytes 16777216 | tf_op jit(solution)/shard_map/begin/pallas_call | solution.py:541
  110.1 39.9 %finish.1 = bf16[3,768,768]{2,1,0:T(8,128)(2,1)} custom-call(s32[3]{0:T(128)} %copy-done.16, s32[2,2]{1,0:T(2,128)} %bitcast.77, bf16[2,512,768]{2,1,0:T(8,128)(2,1)} %copy-done.20, bf16[2,2,128,768]{3,2,1,0:T(8,128)(2,1)} %collective-permute-done.refs_1_, bf16[2,2,128,768]{3,2,1,0:T(8,128)(2,1)} %collective-permute-done.6.refs_2_, ...), custom_call_target="tpu_custom_call" | custom-call | flops 21474836480 | bytes 16777216 | tf_op jit(solution)/shard_map/finish/pallas_call | solution.py:541
  150.1 2.5 %fusion.11 = (bf16[3,128,768]{2,1,0:T(8,128)(2,1)}, bf16[3,128,768]{2,1,0:T(8,128)(2,1)}) fusion(bf16[3,768,768]{2,1,0:T(8,128)(2,1)} %finish.1), kind=kLoop, calls=%fused_computation.48 | loop fusion | bytes 2359296 | tf_op jit(solution)/shard_map/slice | solution.py:587
  153.1 1.9 %collective-permute-done.19 = bf16[3,128,768]{2,1,0:T(8,128)(2,1)} collective-permute-done((bf16[3,128,768]{2,1,0:T(8,128)(2,1)}, bf16[3,128,768]{2,1,0:T(8,128)(2,1)}, u32[]{:S(2)}, u32[]{:S(2)}) %collective-permute-start.19) | collective-permute-done | bytes 589856 | tf_op jit(solution)/shard_map/ppermute | solution.py:587
  155.0 0.8 collective-permute-done.20
  155.9 1.5 add_convert_fusion.1
  158.3 2.2 %collective-permute-start.21 = (bf16[3,2,128,384]{3,2,0,1:T(8,128)(2,1)S(1)}, bf16[3,2,128,384]{3,2,0,1:T(8,128)(2,1)S(1)}, u32[]{:S(2)}, u32[]{:S(2)}) collective-permute-start(bf16[3,2,128,384]{3,2,0,1:T(8,128)(2,1)S(1)} %bitcast.74), channel_id=1, source_target_pairs={{0,2},{1,3},{2,0},{3,1},{4,6},{5,7},{6,4},{7,5},{8,10},{9,11},{10,... | collective-permute-start | bytes 1769480 | tf_op jit(solution)/shard_map/ppermute | solution.py:24
  160.5 13.2 %collective-permute-done.23 = bf16[3,2,128,384]{3,2,0,1:T(8,128)(2,1)S(1)} collective-permute-done((bf16[3,2,128,384]{3,2,0,1:T(8,128)(2,1)S(1)}, bf16[3,2,128,384]{3,2,0,1:T(8,128)(2,1)S(1)}, u32[]{:S(2)}, u32[]{:S(2)}) %collective-permute-start.23) | collective-permute-done | bytes 589856 | tf_op jit(solution)/shard_map/ppermute | solution.py:24
  174.5 1.8 collective-permute-start.22
  176.3 6.1 %collective-permute-done.24 = bf16[3,128,384]{2,1,0:T(8,128)(2,1)S(1)} collective-permute-done((bf16[3,128,384]{2,1,0:T(8,128)(2,1)S(1)}, bf16[3,128,384]{2,1,0:T(8,128)(2,1)S(1)}, u32[]{:S(2)}, u32[]{:S(2)}) %collective-permute-start.24) | collective-permute-done | bytes 294944 | tf_op jit(solution)/shard_map/ppermute | solution.py:24
  183.1 2.2 %fusion.3 = f32[1,2,128,768]{3,2,1,0:T(8,128)} fusion(f32[3,128,384]{2,1,0:T(8,128)S(1)} %bitcast_add_fusion.1, f32[3,128,384]{2,1,0:T(8,128)S(1)} %bitcast_add_fusion, f32[1,2,512,768]{3,2,1,0:T(8,128)} %param.9, s32[]{:T(128)S(6)} %select_n.23, f32[128,768]{1,0:T(8,128)S(1)} %fusion.5), kind=kLoop, calls=%fused_computation.13 | loop fusion | flops 589824 | bytes 3145732 | tf_op jit(solution)/shard_map/broadcast_in_dim | solution.py:605
  (96 shorter events, 9.3 us)
Async XLA Ops:
  1.9 21.9 %collective-permute-start.7 = (bf16[2,128,768]{2,1,0:T(8,128)(2,1)}, bf16[2,128,768]{2,1,0:T(8,128)(2,1)S(1)}, u32[]{:S(2)}, u32[]{:S(2)}) collective-permute-start(bf16[2,128,768]{2,1,0:T(8,128)(2,1)} %bitcast_convert_fusion), channel_id=1, source_target_pairs={{0,16},{8,24},{16,0},{24,8},{1,17},{9,25},{17,1},{25,9},{2,18},{10... | collective-permute-start | bytes 1179656 | tf_op jit(solution)/shard_map/ppermute | solution.py:24
  6.0 22.6 %collective-permute-start.1 = (bf16[2,128,768]{2,1,0:T(8,128)(2,1)}, bf16[2,128,768]{2,1,0:T(8,128)(2,1)S(1)}, u32[]{:S(2)}, u32[]{:S(2)}) collective-permute-start(bf16[2,128,768]{2,1,0:T(8,128)(2,1)} %bitcast_convert_fusion), channel_id=1, source_target_pairs={{0,8},{8,0},{16,24},{24,16},{1,9},{9,1},{17,25},{25,17},{2,10},{10... | collective-permute-start | bytes 1179656 | tf_op jit(solution)/shard_map/ppermute | solution.py:24
  9.6 3.8 %copy-start.20 = (bf16[2,512,768]{2,1,0:T(8,128)(2,1)}, bf16[2,512,768]{2,1,0:T(8,128)(2,1)S(1)}, u32[]{:S(2)}) copy-start(bf16[2,512,768]{2,1,0:T(8,128)(2,1)S(1)} %convert_bitcast_fusion.refs_0_) | copy-start | bytes 4718596
  12.5 15.3 %copy-start.18 = (bf16[1,512,512]{1,2,0:T(8,128)(2,1)}, bf16[1,512,512]{1,2,0:T(8,128)(2,1)S(1)}, u32[]{:S(2)}) copy-start(bf16[1,512,512]{1,2,0:T(8,128)(2,1)S(1)} %copy.24) | copy-start | bytes 1572868
  12.5 1.7 copy-start.21
  23.8 27.7 %copy-start.6 = (bf16[2,128,768]{2,1,0:T(8,128)(2,1)}, bf16[2,128,768]{2,1,0:T(8,128)(2,1)S(1)}, u32[]{:S(2)}) copy-start(bf16[2,128,768]{2,1,0:T(8,128)(2,1)S(1)} %collective-permute-done.7.refs_0_.refs_9_.refs_10_) | copy-start | bytes 1179652
  23.8 12.0 %collective-permute-start.8 = (bf16[2,128,768]{2,1,0:T(8,128)(2,1)S(1)}, bf16[2,128,768]{2,1,0:T(8,128)(2,1)S(1)}, u32[]{:S(2)}, u32[]{:S(2)}) collective-permute-start(bf16[2,128,768]{2,1,0:T(8,128)(2,1)S(1)} %collective-permute-done.7.refs_0_.refs_9_.refs_10_), channel_id=1, source_target_pairs={{0,1},{1,0},{2,3},{3,2},{4,5},{5,4},{6,7},{7,6},{8,9},{9,8},{10,11... | collective-permute-start | bytes 1179656 | tf_op jit(solution)/shard_map/ppermute | solution.py:24
  26.2 12.0 %collective-permute-start.9 = (bf16[2,128,768]{2,1,0:T(8,128)(2,1)S(1)}, bf16[2,128,768]{2,1,0:T(8,128)(2,1)S(1)}, u32[]{:S(2)}, u32[]{:S(2)}) collective-permute-start(bf16[2,128,768]{2,1,0:T(8,128)(2,1)S(1)} %collective-permute-done.7.refs_0_.refs_9_.refs_10_), channel_id=1, source_target_pairs={{0,2},{1,3},{2,0},{3,1},{4,6},{5,7},{6,4},{7,5},{8,10},{9,11},{10,... | collective-permute-start | bytes 1179656 | tf_op jit(solution)/shard_map/ppermute | solution.py:24
  28.6 25.1 %copy-start.8 = (bf16[2,128,768]{2,1,0:T(8,128)(2,1)}, bf16[2,128,768]{2,1,0:T(8,128)(2,1)S(1)}, u32[]{:S(2)}) copy-start(bf16[2,128,768]{2,1,0:T(8,128)(2,1)S(1)} %collective-permute-done.1.refs_0_.refs_4_.refs_5_) | copy-start | bytes 1179652
  28.6 15.7 %collective-permute-start.2 = (bf16[2,128,768]{2,1,0:T(8,128)(2,1)S(1)}, bf16[2,128,768]{2,1,0:T(8,128)(2,1)S(1)}, u32[]{:S(2)}, u32[]{:S(2)}) collective-permute-start(bf16[2,128,768]{2,1,0:T(8,128)(2,1)S(1)} %collective-permute-done.1.refs_0_.refs_4_.refs_5_), channel_id=1, source_target_pairs={{0,1},{1,0},{2,3},{3,2},{4,5},{5,4},{6,7},{7,6},{8,9},{9,8},{10,11... | collective-permute-start | bytes 1179656 | tf_op jit(solution)/shard_map/ppermute | solution.py:24
  29.1 17.5 %collective-permute-start.3 = (bf16[2,128,768]{2,1,0:T(8,128)(2,1)S(1)}, bf16[2,128,768]{2,1,0:T(8,128)(2,1)S(1)}, u32[]{:S(2)}, u32[]{:S(2)}) collective-permute-start(bf16[2,128,768]{2,1,0:T(8,128)(2,1)S(1)} %collective-permute-done.1.refs_0_.refs_4_.refs_5_), channel_id=1, source_target_pairs={{0,2},{1,3},{2,0},{3,1},{4,6},{5,7},{6,4},{7,5},{8,10},{9,11},{10,... | collective-permute-start | bytes 1179656 | tf_op jit(solution)/shard_map/ppermute | solution.py:24
  29.6 19.2 %collective-permute-start.13 = (bf16[2,128,768]{2,1,0:T(8,128)(2,1)S(1)}, bf16[2,128,768]{2,1,0:T(8,128)(2,1)}, u32[]{:S(2)}, u32[]{:S(2)}) collective-permute-start(bf16[2,128,768]{2,1,0:T(8,128)(2,1)S(1)} %collective-permute-done.7.refs_0_.refs_9_.refs_10_), channel_id=1, source_target_pairs={{0,8},{8,0},{16,24},{24,16},{1,9},{9,1},{17,25},{25,17},{2,10},{10... | collective-permute-start | bytes 1179656 | tf_op jit(solution)/shard_map/ppermute | solution.py:24
  35.8 20.2 %copy-start = (bf16[2,128,768]{2,1,0:T(8,128)(2,1)}, bf16[2,128,768]{2,1,0:T(8,128)(2,1)S(1)}, u32[]{:S(2)}) copy-start(bf16[2,128,768]{2,1,0:T(8,128)(2,1)S(1)} %collective-permute-done.8.refs_1_.refs_10_.refs_11_) | copy-start | bytes 1179652
  35.8 17.9 %collective-permute-start.10 = (bf16[128,768]{1,0:T(8,128)(2,1)S(1)}, bf16[128,768]{1,0:T(8,128)(2,1)S(1)}, u32[]{:S(2)}, u32[]{:S(2)}) collective-permute-start(bf16[128,768]{1,0:T(8,128)(2,1)S(1)} %slice_bitcast_fusion.7), channel_id=1, source_target_pairs={{0,2},{1,3},{2,0},{3,1},{4,6},{5,7},{6,4},{7,5},{8,10},{9,11},{10,... | collective-permute-start | bytes 589832 | tf_op jit(solution)/shard_map/ppermute | solution.py:24
  38.2 21.1 %copy-start.1 = (bf16[2,128,768]{2,1,0:T(8,128)(2,1)}, bf16[2,128,768]{2,1,0:T(8,128)(2,1)S(1)}, u32[]{:S(2)}) copy-start(bf16[2,128,768]{2,1,0:T(8,128)(2,1)S(1)} %collective-permute-done.9.refs_2_.refs_11_.refs_12_) | copy-start | bytes 1179652
  38.9 14.9 %collective-permute-start.11 = (bf16[128,768]{1,0:T(8,128)(2,1)}, bf16[128,768]{1,0:T(8,128)(2,1)S(1)}, u32[]{:S(2)}, u32[]{:S(2)}) collective-permute-start(bf16[128,768]{1,0:T(8,128)(2,1)} %slice_bitcast_fusion.6), channel_id=1, source_target_pairs={{0,1},{1,0},{2,3},{3,2},{4,5},{5,4},{6,7},{7,6},{8,9},{9,8},{10,11... | collective-permute-start | bytes 589832 | tf_op jit(solution)/shard_map/ppermute | solution.py:24
  44.3 15.3 %copy-start.2 = (bf16[2,128,768]{2,1,0:T(8,128)(2,1)}, bf16[2,128,768]{2,1,0:T(8,128)(2,1)S(1)}, u32[]{:S(2)}) copy-start(bf16[2,128,768]{2,1,0:T(8,128)(2,1)S(1)} %collective-permute-done.2.refs_1_.refs_5_.refs_6_) | copy-start | bytes 1179652
  45.0 14.3 %collective-permute-start.4 = (bf16[128,768]{1,0:T(8,128)(2,1)}, bf16[128,768]{1,0:T(8,128)(2,1)}, u32[]{:S(2)}, u32[]{:S(2)}) collective-permute-start(bf16[128,768]{1,0:T(8,128)(2,1)} %slice_bitcast_fusion.9), channel_id=1, source_target_pairs={{0,2},{1,3},{2,0},{3,1},{4,6},{5,7},{6,4},{7,5},{8,10},{9,11},{10,... | collective-permute-start | bytes 589832 | tf_op jit(solution)/shard_map/ppermute | solution.py:24
  46.6 12.9 %copy-start.3 = (bf16[2,128,768]{2,1,0:T(8,128)(2,1)}, bf16[2,128,768]{2,1,0:T(8,128)(2,1)S(1)}, u32[]{:S(2)}) copy-start(bf16[2,128,768]{2,1,0:T(8,128)(2,1)S(1)} %collective-permute-done.3.refs_2_.refs_6_.refs_7_) | copy-start | bytes 1179652
  47.4 12.2 %collective-permute-start.5 = (bf16[128,768]{1,0:T(8,128)(2,1)}, bf16[128,768]{1,0:T(8,128)(2,1)}, u32[]{:S(2)}, u32[]{:S(2)}) collective-permute-start(bf16[128,768]{1,0:T(8,128)(2,1)} %slice_bitcast_fusion.8), channel_id=1, source_target_pairs={{0,1},{1,0},{2,3},{3,2},{4,5},{5,4},{6,7},{7,6},{8,9},{9,8},{10,11... | collective-permute-start | bytes 589832 | tf_op jit(solution)/shard_map/ppermute | solution.py:24
  48.8 19.5 %collective-permute-start.14 = (bf16[2,128,768]{2,1,0:T(8,128)(2,1)}, bf16[2,128,768]{2,1,0:T(8,128)(2,1)S(1)}, u32[]{:S(2)}, u32[]{:S(2)}) collective-permute-start(bf16[2,128,768]{2,1,0:T(8,128)(2,1)} %collective-permute-done.13.refs_0_.refs_15_), channel_id=1, source_target_pairs={{0,1},{1,0},{2,3},{3,2},{4,5},{5,4},{6,7},{7,6},{8,9},{9,8},{10,11... | collective-permute-start | bytes 1179656 | tf_op jit(solution)/shard_map/ppermute | solution.py:24
  49.5 30.2 %copy-start.16 = (s32[3]{0:T(128)}, s32[3]{0:T(128)S(1)}, u32[]{:S(2)}) copy-start(s32[3]{0:T(128)S(1)} %pad_add_fusion.info) | copy-start | bytes 40
  51.5 10.2 %copy-start.19 = (bf16[1,512,512]{1,2,0:T(8,128)(2,1)S(1)}, bf16[1,512,512]{1,2,0:T(8,128)(2,1)}, u32[]{:S(2)}) copy-start(bf16[1,512,512]{1,2,0:T(8,128)(2,1)} %copy-done.18) | copy-start | bytes 1572868
  51.5 10.2 %copy-start.23 = (bf16[512,512]{0,1:T(8,128)(2,1)S(1)}, bf16[512,512]{0,1:T(8,128)(2,1)}, u32[]{:S(2)}) copy-start(bf16[512,512]{0,1:T(8,128)(2,1)} %bitcast_negate_fusion) | copy-start | bytes 1572868
  51.5 10.2 %copy-start.24 = (bf16[1,512,512]{1,2,0:T(8,128)(2,1)S(1)}, bf16[1,512,512]{1,2,0:T(8,128)(2,1)}, u32[]{:S(2)}) copy-start(bf16[1,512,512]{1,2,0:T(8,128)(2,1)} %copy.23) | copy-start | bytes 1572868
  53.7 5.8 %copy-start.10 = (bf16[128,768]{1,0:T(8,128)(2,1)}, bf16[128,768]{1,0:T(8,128)(2,1)S(1)}, u32[]{:S(2)}) copy-start(bf16[128,768]{1,0:T(8,128)(2,1)S(1)} %collective-permute-done.10.refs_3_.refs_12_.refs_13_) | copy-start | bytes 589828
  53.7 29.3 %collective-permute-start = (bf16[2,2,128,768]{3,2,1,0:T(8,128)(2,1)}, bf16[2,2,128,768]{3,2,1,0:T(8,128)(2,1)}, u32[]{:S(2)}, u32[]{:S(2)}) collective-permute-start(bf16[2,2,128,768]{3,2,1,0:T(8,128)(2,1)} %pad_maximum_fusion.1), channel_id=1, source_target_pairs={{0,4},{4,0},{1,5},{5,1},{2,6},{6,2},{3,7},{7,3},{8,12},{12,8},{9,1... | collective-permute-start | bytes 2359304 | tf_op jit(solution)/shard_map/ppermute | solution.py:111
  54.5 14.6 %collective-permute-start.15 = (bf16[2,128,768]{2,1,0:T(8,128)(2,1)}, bf16[2,128,768]{2,1,0:T(8,128)(2,1)S(1)}, u32[]{:S(2)}, u32[]{:S(2)}) collective-permute-start(bf16[2,128,768]{2,1,0:T(8,128)(2,1)} %collective-permute-done.13.refs_0_.refs_15_), channel_id=1, source_target_pairs={{0,2},{1,3},{2,0},{3,1},{4,6},{5,7},{6,4},{7,5},{8,10},{9,11},{10,... | collective-permute-start | bytes 1179656 | tf_op jit(solution)/shard_map/ppermute | solution.py:24
  56.0 1.0 copy-start.7
  57.0 0.9 copy-start.12
  58.0 1.6 copy-start.9
  59.3 23.7 %collective-permute-start.12 = (bf16[2,2,128,768]{3,2,1,0:T(8,128)(2,1)S(1)}, bf16[2,2,128,768]{3,2,1,0:T(8,128)(2,1)}, u32[]{:S(2)}, u32[]{:S(2)}) collective-permute-start(bf16[2,2,128,768]{3,2,1,0:T(8,128)(2,1)S(1)} %edges.4), channel_id=1, source_target_pairs={{0,4},{4,0},{1,5},{5,1},{2,6},{6,2},{3,7},{7,3},{8,12},{12,8},{9,1... | collective-permute-start | bytes 2359304 | tf_op jit(solution)/shard_map/ppermute | solution.py:111
  61.4 21.6 %collective-permute-start.6 = (bf16[2,2,128,768]{3,2,1,0:T(8,128)(2,1)S(1)}, bf16[2,2,128,768]{3,2,1,0:T(8,128)(2,1)}, u32[]{:S(2)}, u32[]{:S(2)}) collective-permute-start(bf16[2,2,128,768]{3,2,1,0:T(8,128)(2,1)S(1)} %edges.3), channel_id=1, source_target_pairs={{0,4},{4,0},{1,5},{5,1},{2,6},{6,2},{3,7},{7,3},{8,12},{12,8},{9,1... | collective-permute-start | bytes 2359304 | tf_op jit(solution)/shard_map/ppermute | solution.py:111
  64.3 7.4 %copy-start.22 = (bf16[512,512]{1,0:T(8,128)(2,1)S(1)}, bf16[512,512]{1,0:T(8,128)(2,1)}, u32[]{:S(2)}) copy-start(bf16[512,512]{1,0:T(8,128)(2,1)} %fusion.8) | copy-start | bytes 1572868
  68.3 11.4 %copy-start.4 = (bf16[2,128,768]{2,1,0:T(8,128)(2,1)}, bf16[2,128,768]{2,1,0:T(8,128)(2,1)S(1)}, u32[]{:S(2)}) copy-start(bf16[2,128,768]{2,1,0:T(8,128)(2,1)S(1)} %collective-permute-done.14.refs_1_.refs_16_) | copy-start | bytes 1179652
  69.1 10.6 %collective-permute-start.16 = (bf16[128,768]{1,0:T(8,128)(2,1)}, bf16[128,768]{1,0:T(8,128)(2,1)S(1)}, u32[]{:S(2)}, u32[]{:S(2)}) collective-permute-start(bf16[128,768]{1,0:T(8,128)(2,1)} %slice_bitcast_fusion.5), channel_id=1, source_target_pairs={{0,2},{1,3},{2,0},{3,1},{4,6},{5,7},{6,4},{7,5},{8,10},{9,11},{10,... | collective-permute-start | bytes 589832 | tf_op jit(solution)/shard_map/ppermute | solution.py:24
  69.1 10.6 %copy-start.5 = (bf16[2,128,768]{2,1,0:T(8,128)(2,1)}, bf16[2,128,768]{2,1,0:T(8,128)(2,1)S(1)}, u32[]{:S(2)}) copy-start(bf16[2,128,768]{2,1,0:T(8,128)(2,1)S(1)} %collective-permute-done.15.refs_2_.refs_17_) | copy-start | bytes 1179652
  69.8 9.8 %collective-permute-start.17 = (bf16[128,768]{1,0:T(8,128)(2,1)}, bf16[128,768]{1,0:T(8,128)(2,1)S(1)}, u32[]{:S(2)}, u32[]{:S(2)}) collective-permute-start(bf16[128,768]{1,0:T(8,128)(2,1)} %slice_bitcast_fusion.4), channel_id=1, source_target_pairs={{0,1},{1,0},{2,3},{3,2},{4,5},{5,4},{6,7},{7,6},{8,9},{9,8},{10,11... | collective-permute-start | bytes 589832 | tf_op jit(solution)/shard_map/ppermute | solution.py:24
  79.7 30.4 %copy-start.13 = (bf16[128,768]{1,0:T(8,128)(2,1)}, bf16[128,768]{1,0:T(8,128)(2,1)S(1)}, u32[]{:S(2)}) copy-start(bf16[128,768]{1,0:T(8,128)(2,1)S(1)} %collective-permute-done.16.refs_3_.refs_18_) | copy-start | bytes 589828
  82.9 27.2 %collective-permute-start.18 = (bf16[2,2,128,768]{3,2,1,0:T(8,128)(2,1)S(1)}, bf16[2,2,128,768]{3,2,1,0:T(8,128)(2,1)}, u32[]{:S(2)}, u32[]{:S(2)}) collective-permute-start(bf16[2,2,128,768]{3,2,1,0:T(8,128)(2,1)S(1)} %edges.5), channel_id=1, source_target_pairs={{0,4},{4,0},{1,5},{5,1},{2,6},{6,2},{3,7},{7,3},{8,12},{12,8},{9,1... | collective-permute-start | bytes 2359304 | tf_op jit(solution)/shard_map/ppermute | solution.py:111
  150.1 5.8 %copy-start.17 = (bf16[3,768,768]{2,1,0:T(8,128)(2,1)S(1)}, bf16[3,768,768]{2,1,0:T(8,128)(2,1)}, u32[]{:S(2)}) copy-start(bf16[3,768,768]{2,1,0:T(8,128)(2,1)} %finish.1) | copy-start | bytes 10616836
  152.6 2.4 %collective-permute-start.19 = (bf16[3,128,768]{2,1,0:T(8,128)(2,1)}, bf16[3,128,768]{2,1,0:T(8,128)(2,1)}, u32[]{:S(2)}, u32[]{:S(2)}) collective-permute-start(bf16[3,128,768]{2,1,0:T(8,128)(2,1)} %get-tuple-element.13), channel_id=1, source_target_pairs={{0,4},{4,0},{1,5},{5,1},{2,6},{6,2},{3,7},{7,3},{8,12},{12,8},{9,1... | collective-permute-start | bytes 1769480 | tf_op jit(solution)/shard_map/ppermute | solution.py:587
  153.1 2.8 %collective-permute-start.20 = (bf16[3,128,768]{2,1,0:T(8,128)(2,1)}, bf16[3,128,768]{2,1,0:T(8,128)(2,1)}, u32[]{:S(2)}, u32[]{:S(2)}) collective-permute-start(bf16[3,128,768]{2,1,0:T(8,128)(2,1)} %get-tuple-element.14), channel_id=1, source_target_pairs={{0,4},{4,0},{1,5},{5,1},{2,6},{6,2},{3,7},{7,3},{8,12},{12,8},{9,1... | collective-permute-start | bytes 1769480 | tf_op jit(solution)/shard_map/ppermute | solution.py:588
  153.1 4.3 %slice-start = ((bf16[3,768,768]{2,1,0:T(8,128)(2,1)}), bf16[3,256,768]{2,1,0:T(8,128)(2,1)S(1)}, s32[]{:S(2)}) async-start(bf16[3,768,768]{2,1,0:T(8,128)(2,1)} %finish.1), calls=%async_computation | async-start | bytes 2359296 | tf_op jit(solution)/shard_map/slice | solution.py:592
  158.0 15.7 %collective-permute-start.23 = (bf16[3,2,128,384]{3,2,0,1:T(8,128)(2,1)S(1)}, bf16[3,2,128,384]{3,2,0,1:T(8,128)(2,1)S(1)}, u32[]{:S(2)}, u32[]{:S(2)}) collective-permute-start(bf16[3,2,128,384]{3,2,0,1:T(8,128)(2,1)S(1)} %bitcast.73), channel_id=1, source_target_pairs={{0,1},{1,0},{2,3},{3,2},{4,5},{5,4},{6,7},{7,6},{8,9},{9,8},{10,11... | collective-permute-start | bytes 1769480 | tf_op jit(solution)/shard_map/ppermute | solution.py:24
  158.3 16.0 %collective-permute-start.21 = (bf16[3,2,128,384]{3,2,0,1:T(8,128)(2,1)S(1)}, bf16[3,2,128,384]{3,2,0,1:T(8,128)(2,1)S(1)}, u32[]{:S(2)}, u32[]{:S(2)}) collective-permute-start(bf16[3,2,128,384]{3,2,0,1:T(8,128)(2,1)S(1)} %bitcast.74), channel_id=1, source_target_pairs={{0,2},{1,3},{2,0},{3,1},{4,6},{5,7},{6,4},{7,5},{8,10},{9,11},{10,... | collective-permute-start | bytes 1769480 | tf_op jit(solution)/shard_map/ppermute | solution.py:24
  173.9 8.5 %collective-permute-start.24 = (bf16[3,128,384]{2,1,0:T(8,128)(2,1)S(1)}, bf16[3,128,384]{2,1,0:T(8,128)(2,1)S(1)}, u32[]{:S(2)}, u32[]{:S(2)}) collective-permute-start(bf16[3,128,384]{2,1,0:T(8,128)(2,1)S(1)} %fusion.7), channel_id=1, source_target_pairs={{0,2},{1,3},{2,0},{3,1},{4,6},{5,7},{6,4},{7,5},{8,10},{9,11},{10,... | collective-permute-start | bytes 884744 | tf_op jit(solution)/shard_map/ppermute | solution.py:24
  174.5 8.5 %collective-permute-start.22 = (bf16[3,128,384]{2,1,0:T(8,128)(2,1)S(1)}, bf16[3,128,384]{2,1,0:T(8,128)(2,1)S(1)}, u32[]{:S(2)}, u32[]{:S(2)}) collective-permute-start(bf16[3,128,384]{2,1,0:T(8,128)(2,1)S(1)} %fusion.6), channel_id=1, source_target_pairs={{0,1},{1,0},{2,3},{3,2},{4,5},{5,4},{6,7},{7,6},{8,9},{9,8},{10,11... | collective-permute-start | bytes 884744 | tf_op jit(solution)/shard_map/ppermute | solution.py:24
  (3 other events, 2.3 us)
